TPU v7x, 128 devices: a whole 4x4x4 slice. The times are simulated.
128 devices in a mesh: ctx: 16 (over y, z_hi, core), dp: 8 (over x, z_lo).
Axes of the slice: x: 4, y: 4, z: 4 (z_hi: 2, z_lo: 2; z = z_hi * 2 + z_lo), core: 2. Of those that a mesh axis runs over, the one named last changes fastest.
Arguments:
- tokens: bfloat16 [8, 4096, 16384], P('dp', 'ctx'), may hold values from -6 to 6
- queries: bfloat16 [8, 4096, 1024], P('dp', 'ctx'), may hold values from -200 to 200
- cotangent: bfloat16 [8, 4096, 1024], P('dp', 'ctx'), may hold values from -6 to 6
- latent_key: float32 [16384, 128], P(('ctx', 'dp')), may hold values from -1 to 1
- latent_value: float32 [16384, 128], P(('ctx', 'dp')), may hold values from -1 to 1
- lengths: int32 [8, 8], P('dp'), may hold values from 1 to 2048, 4096 in all within a row
- block_order: int32 [8, 32], P('dp'), may hold values from 0 to 31, each once within a row
Outputs:
- attn_out: bfloat16 [8, 4096, 1024], P('dp', 'ctx')
- query_grad: bfloat16 [8, 4096, 1024], P('dp', 'ctx')
- token_grad: bfloat16 [8, 4096, 16384], P('dp', 'ctx')
- key_weight_grad: float32 [16384, 128], P(('ctx', 'dp'))
- value_weight_grad: float32 [16384, 128], P(('ctx', 'dp'))
Inputs may be any that keep to these rules, and one draw needn't show every extreme that they name: Each row holds the lengths of the 8 documents packed into one sequence, in order; they sum to 4096 and the largest is exactly 2048. Each row is a permutation; stored block b of a sequence (rows b * 128 to (b + 1) * 128 - 1) holds the tokens at positions block_order[b] * 128 to block_order[b] * 128 + 127.
All inputs are finite; a program needn't handle non-finite values. Where the computation divides by a largest or mean magnitude, that divisor is 1e-20 or more.
Results may differ from a plain program's by a relative error of at most 0.02.
The roundings to bfloat16 on the way count: a program that leaves them out, or rounds other values in their place, can miss the bound.
Values may be sent and summed in bfloat16 or wider, within the bound.
No kernel may reach another device: no remote copies, remote signals or barrier semaphores. Data moves between devices by JAX's collectives and lax.ppermute only.
A program may use at most 128 MiB of HBM per device.

v0:
```python
import functools

import jax
import jax.numpy as jnp
import numpy as np
from jax import lax
from jax.experimental import pallas as pl
from jax.experimental.pallas import tpu as pltpu
from jax.sharding import Mesh
from jax.sharding import PartitionSpec as P

AXES = ("y", "zh", "core", "x", "zl")
SIZES = (4, 2, 2, 4, 2)
CTX = ("y", "zh", "core")
DP = ("x", "zl")
SAME_CORE_CTX = ("y", "zh")
DEVICES = int(np.prod(SIZES))

EPSILON = 1e-05
NEGATIVE = -1e30
KEY_CHUNK = 256
STRIP = 32

RING_ORDER = {0: ("x", "y", "z"), 1: ("y", "z", "x")}
OFFSETS = (0, -1, 1, 2)


def coordinates(device):
    y, zh, core, x, zl = (int(v) for v in np.unravel_index(device, SIZES))
    return {"y": y, "z": zh * 2 + zl, "x": x, "core": core}


def device_of(place):
    return int(
        np.ravel_multi_index(
            (place["y"], place["z"] // 2, place["core"], place["x"], place["z"] % 2), SIZES
        )
    )


def moved(change):
    pairs = []
    for device in range(DEVICES):
        place = coordinates(device)
        change(place)
        pairs.append((device, device_of(place)))
    return pairs


def along_ring(phase, step):
    def change(place):
        axis = RING_ORDER[place["core"]][phase]
        place[axis] = (place[axis] + step) % 4

    return moved(change)


def to_other_core(place):
    place["core"] = 1 - place["core"]


def swap_cores(value):
    return lax.ppermute(value, AXES, moved(to_other_core))


def block_table():
    table = np.zeros((DEVICES, DEVICES), np.int32)
    for device in range(DEVICES):
        here = coordinates(device)
        at = 0
        for core in (here["core"], 1 - here["core"]):
            order = RING_ORDER[core]
            for last in OFFSETS:
                for middle in OFFSETS:
                    for first in OFFSETS:
                        place = dict(here, core=core)
                        for axis, step in zip(order, (first, middle, last)):
                            place[axis] = (place[axis] + step) % 4
                        table[device, at] = device_of(place)
                        at += 1
    return table


def gather_ring(value, phase):
    return [value] + [
        lax.ppermute(value, AXES, along_ring(phase, -offset)) for offset in OFFSETS[1:]
    ]


def sent_along_ring(pieces, phase):
    return [
        lax.ppermute(piece.astype(jnp.bfloat16), AXES, along_ring(phase, offset))
        for piece, offset in zip(pieces, OFFSETS[1:])
    ]


def shuffle_kernel(table, tokens, own, other):
    width = own.shape[1] * 2 // DEVICES
    half = DEVICES // 2

    def move(j, _):
        target = pl.ds(pl.multiple_of(j * width, width), width)
        for first, out in ((0, own), (half, other)):
            source = pl.ds(pl.multiple_of(table[first + j] * width, width), width)
            out[:, target] = tokens[:, source]
        return 0

    lax.fori_loop(0, half, move, 0, unroll=8)


def shuffle(table, tokens):
    rows, features = tokens.shape
    step_rows = 32
    half = jax.ShapeDtypeStruct((rows, features // 2), tokens.dtype)
    half_spec = pl.BlockSpec((step_rows, features // 2), lambda i: (i, 0))
    return pl.pallas_call(
        shuffle_kernel,
        grid=(rows // step_rows,),
        out_shape=(half, half),
        in_specs=[
            pl.BlockSpec(memory_space=pltpu.SMEM),
            pl.BlockSpec((step_rows, features), lambda i: (i, 0)),
        ],
        out_specs=(half_spec, half_spec),
        compiler_params=pltpu.CompilerParams(vmem_limit_bytes=16 << 20),
        cost_estimate=pl.CostEstimate(
            flops=0, bytes_accessed=4 * rows * features, transcendentals=0
        ),
        name="shuffle_tokens",
    )(table, tokens)


def weight_terms_kernel(grads, peer_grads, tokens, peer_tokens, *rest, first, count):
    outs, (held_grads, turned, held, made, grad_sems, sems, out_sems) = rest[:count], rest[count:]
    grad_copies = [
        pltpu.make_async_copy(source, held_grads.at[side], grad_sems.at[side])
        for side, source in enumerate((grads, peer_grads))
    ]
    for copy in grad_copies:
        copy.start()
    step = held.shape[2] // (2 * count)
    copies = []
    for n in range(2 * count):
        here, there = slice(n * step, (n + 1) * step), slice(first + n * step, first + (n + 1) * step)
        copies.append(
            [
                pltpu.make_async_copy(source.at[:, there], held.at[side, :, here], sems.at[side, n])
                for side, source in enumerate((tokens, peer_tokens))
            ]
        )
    for pair in copies:
        for copy in pair:
            copy.start()
    for side, copy in enumerate(grad_copies):
        copy.wait()
        turned[side] = held_grads[side].T
    sends = []
    for n, pair in enumerate(copies):
        here = slice(n * step, (n + 1) * step)
        for copy in pair:
            copy.wait()
        term = jnp.dot(turned[0], held[0, :, here], preferred_element_type=jnp.float32) + jnp.dot(
            turned[1], held[1, :, here], preferred_element_type=jnp.float32
        )
        made[:, here] = term.astype(made.dtype)
        sends.append(
            pltpu.make_async_copy(
                made.at[:, here],
                outs[n // 2].at[:, n % 2 * step : (n % 2 + 1) * step],
                out_sems.at[n],
            )
        )
        sends[-1].start()
    for send in sends:
        send.wait()


def weight_terms(grads, peer_grads, tokens, peer_tokens, first, count, dtype):
    rows, features = tokens.shape
    both = grads.shape[1]
    width = features // len(OFFSETS)
    anywhere = pl.BlockSpec(memory_space=pl.ANY)
    return pl.pallas_call(
        functools.partial(weight_terms_kernel, first=first * width, count=count),
        out_shape=(jax.ShapeDtypeStruct((both, width), dtype),) * count,
        in_specs=[anywhere] * 4,
        out_specs=(anywhere,) * count,
        scratch_shapes=[
            pltpu.VMEM((2, rows, both), jnp.bfloat16),
            pltpu.VMEM((2, both, rows), jnp.bfloat16),
            pltpu.VMEM((2, rows, count * width), tokens.dtype),
            pltpu.VMEM((both, count * width), dtype),
            pltpu.SemaphoreType.DMA((2,)),
            pltpu.SemaphoreType.DMA((2, 2 * count)),
            pltpu.SemaphoreType.DMA((2 * count,)),
        ],
        compiler_params=pltpu.CompilerParams(vmem_limit_bytes=58 << 20),
        cost_estimate=pl.CostEstimate(
            flops=4 * rows * both * count * width,
            bytes_accessed=(4 * rows + 2 * both) * count * width,
            transcendentals=0,
        ),
        name="weight_terms",
    )(grads, peer_grads, tokens, peer_tokens)


def pair_kernel(left, right, out, sems):
    width = left.shape[1]
    copies = [
        pltpu.make_async_copy(source, out.at[:, n * width : (n + 1) * width], sems.at[n])
        for n, source in enumerate((left, right))
    ]
    for copy in copies:
        copy.start()
    for copy in copies:
        copy.wait()


def side_by_side(left, right):
    anywhere = pl.BlockSpec(memory_space=pl.ANY)
    return pl.pallas_call(
        pair_kernel,
        out_shape=jax.ShapeDtypeStruct((left.shape[0], 2 * left.shape[1]), left.dtype),
        in_specs=[anywhere, anywhere],
        out_specs=pl.BlockSpec(memory_space=pltpu.VMEM),
        scratch_shapes=[pltpu.SemaphoreType.DMA((2,))],
        compiler_params=pltpu.CompilerParams(vmem_limit_bytes=58 << 20),
        name="pair_latents",
    )(left, right)


def magnitudes_kernel(*refs):
    pieces, out = refs[:-1], refs[-1]
    out[...] = sum(
        jnp.sum(jnp.abs(piece[...]).reshape(-1, *out.shape), axis=0) for piece in pieces
    )


def ternary_kernel(sums, *refs, entries):
    pieces, out = refs[:-1], refs[-1]
    half = out.shape[1] // 2
    for columns in (slice(0, half), slice(half, 2 * half)):
        scale = jnp.sum(sums[:, columns]) / entries + EPSILON
        level = jnp.full((1, half), scale, jnp.float32)
        for n, piece in enumerate(pieces):
            rows = piece.shape[0]
            latent = piece[:, columns]
            out[n * rows : (n + 1) * rows, columns] = jnp.where(
                latent >= 0.5 * level, level, jnp.where(latent <= -0.5 * level, -level, 0.0)
            ).astype(jnp.bfloat16)


def last_sum_kernel(own, first, second, third, key_out, value_out):
    total = own[...]
    for piece in (first, second, third):
        total = total + piece[...].astype(jnp.float32)
    half = key_out.shape[1]
    key_out[...] = total[:half].T
    value_out[...] = total[half:].T


def small(kernel, name, out_shape, *args):
    in_vmem = pl.BlockSpec(memory_space=pltpu.VMEM)
    return pl.pallas_call(
        kernel,
        out_shape=out_shape,
        in_specs=[in_vmem] * len(args),
        out_specs=jax.tree.map(lambda _: in_vmem, out_shape),
        compiler_params=pltpu.CompilerParams(vmem_limit_bytes=12 << 20),
        cost_estimate=pl.CostEstimate(
            flops=0, bytes_accessed=sum(a.size * a.dtype.itemsize for a in args), transcendentals=0
        ),
        name=name,
    )(*args)


def token_grad_kernel(table, grads, *rest, count):
    weights, out = rest[:count], rest[count]
    held, held_sems, buffers, sems = rest[count + 1 :]
    slots, step_width = held.shape[:2]
    width = out.shape[1] // DEVICES
    per_step = step_width // width
    steps_each = weights[0].shape[0] // step_width

    def fetch(step):
        part = (step % steps_each) * step_width
        return pltpu.make_async_copy(
            weights[step // steps_each].at[part : part + step_width, :],
            held.at[step % slots],
            held_sems.at[step % slots],
        )

    for step in range(slots - 1):
        fetch(step).start()
    for step in range(count * steps_each):
        slot = step % 2
        buffer, sem = buffers.at[slot], sems.at[slot]
        if step + slots - 1 < count * steps_each:
            fetch(step + slots - 1).start()
        fetch(step).wait()
        if step >= 2:
            pltpu.make_async_copy(buffer, buffer, sem).wait()
        buffers[slot] = lax.dot_general(
            grads[...],
            held[step % slots],
            (((1,), (1,)), ((), ())),
            preferred_element_type=jnp.float32,
        ).astype(jnp.bfloat16)
        for j in range(per_step):
            target = pl.ds(pl.multiple_of(table[step * per_step + j] * width, width), width)
            pltpu.make_async_copy(
                buffer.at[:, j * width : (j + 1) * width], out.at[:, target], sem
            ).start()
    for slot in range(2):
        pltpu.make_async_copy(buffers.at[slot], buffers.at[slot], sems.at[slot]).wait()


def token_gradient(table, grads, weights):
    rows, both = grads.shape
    features = sum(w.shape[0] for w in weights)
    step_width = 1024
    slots = 4
    return pl.pallas_call(
        functools.partial(token_grad_kernel, count=len(weights)),
        out_shape=jax.ShapeDtypeStruct((rows, features), jnp.bfloat16),
        in_specs=[
            pl.BlockSpec(memory_space=pltpu.SMEM),
            pl.BlockSpec(memory_space=pltpu.VMEM),
        ]
        + [pl.BlockSpec(memory_space=pltpu.HBM)] * len(weights),
        out_specs=pl.BlockSpec(memory_space=pl.ANY),
        scratch_shapes=[
            pltpu.VMEM((slots, step_width, both), jnp.bfloat16),
            pltpu.SemaphoreType.DMA((slots,)),
            pltpu.VMEM((2, rows, step_width), jnp.bfloat16),
            pltpu.SemaphoreType.DMA((2,)),
        ],
        compiler_params=pltpu.CompilerParams(vmem_limit_bytes=58 << 20),
        cost_estimate=pl.CostEstimate(
            flops=2 * rows * both * features,
            bytes_accessed=2 * features * (rows + both),
            transcendentals=0,
        ),
        name="token_gradient",
    )(table, grads, *weights)


def attention_kernel(
    meta, queries, cotangent, peer_both, kv_same, kv_other,
    mixed_out, query_grad, same_out, other_out,
    q_held, c_held, peer_held, kv_held, key_acc, value_acc, scores, prob_grad, low,
    q_columns, c_columns, q_rows, c_rows, sems,
    *, heads, head_size, block, docs, blocks,
):
    scale = head_size ** (-0.5)
    columns = heads * block
    ctx, core = meta[docs + blocks], meta[docs + blocks + 1]
    own_blocks = q_held.shape[0] // block
    in_strip = lax.broadcasted_iota(jnp.int32, (STRIP, columns), 0)
    sides = ((kv_same, core, same_out), (kv_other, 1 - core, other_out))

    def rows_at(index, size):
        return pl.ds(pl.multiple_of(index * size, size), size)

    def true_block(core_of, j):
        return meta[docs + ((j // 2) * 2 + core_of) * 2 + j % 2]

    copies = [
        pltpu.make_async_copy(source, held, sems.at[n])
        for n, (source, held) in enumerate(
            ((queries, q_held), (cotangent, c_held), (peer_both, peer_held))
        )
    ]
    for copy in copies:
        copy.start()
    for n, (ref, core_of, _) in enumerate(sides):
        for j in range(blocks // 2):
            pltpu.make_async_copy(
                ref.at[j * block : (j + 1) * block, :],
                kv_held.at[rows_at(true_block(core_of, j) + 1, block), :],
                sems.at[len(copies) + n],
            ).start()
    kv_held[:block, :] = jnp.zeros((block, 2 * head_size), kv_held.dtype)
    key_acc[...] = jnp.zeros_like(key_acc)
    value_acc[...] = jnp.zeros_like(value_acc)
    for copy in copies:
        copy.wait()
    for i in range(2 * own_blocks):
        here = slice(i % own_blocks * block, (i % own_blocks + 1) * block)
        for h in range(heads):
            part = slice(h * block, (h + 1) * block)
            if i < own_blocks:
                head = rows_at(core * heads + h, head_size)
                q, c = q_held[here, head], c_held[here, head]
            else:
                q = peer_held[here, h * head_size : (h + 1) * head_size]
                c = peer_held[here, (heads + h) * head_size : (heads + h + 1) * head_size]
            q_rows[i, part, :], c_rows[i, part, :] = q, c
            q_columns[i, :, part], c_columns[i, :, part] = q.T, c.T
    for n, (ref, _, _) in enumerate(sides):
        pltpu.make_async_copy(
            ref, kv_held.at[: blocks // 2 * block, :], sems.at[len(copies) + n]
        ).wait()

    def chunk_rows(last, c):
        return pl.ds(pl.multiple_of((last - 2 * c) * block, block), 2 * block)

    def one_block(i, _):
        here = rows_at(i, block)
        ctx_of = jnp.where(i < own_blocks, ctx, ctx + 1 - 2 * core)
        last = meta[docs + own_blocks * ctx_of + lax.rem(i, own_blocks)]
        start = last * block
        position = start + lax.rem(lax.broadcasted_iota(jnp.int32, (1, columns), 1), block)
        own_start = jnp.zeros((1, columns), jnp.int32)
        first = jnp.int32(0)
        for d in range(docs):
            doc_start = meta[d]
            own_start = jnp.maximum(own_start, jnp.where(position >= doc_start, doc_start, 0))
            first = jnp.maximum(first, jnp.where(start >= doc_start, doc_start, 0))
        count = (last - first // block) // 2 + 1

        def score(c, best):
            scores[c] = jnp.dot(
                kv_held[chunk_rows(last, c), :head_size],
                q_columns[i],
                preferred_element_type=jnp.float32,
            )
            first_key = (last - 2 * c - 1) * block
            for at in range(0, KEY_CHUNK, STRIP):
                strip = slice(at, at + STRIP)
                key_pos = first_key + at + in_strip
                visible = (key_pos >= own_start) & (key_pos <= position)
                s = jnp.where(visible, scores[c, strip, :] * scale, NEGATIVE)
                scores[c, strip, :] = s
                best = jnp.maximum(best, jnp.max(s.reshape(STRIP // 8, 8, columns), axis=0))
            return best

        best = lax.fori_loop(
            0, count, score, jnp.full((8, columns), NEGATIVE, jnp.float32)
        )
        best = jnp.max(best, axis=0, keepdims=True)

        def mix(c, carried):
            total, acc = carried
            for at in range(0, KEY_CHUNK, STRIP):
                strip = slice(at, at + STRIP)
                w = jnp.exp(scores[c, strip, :] - best)
                scores[c, strip, :] = w
                low[0, strip, :] = w.astype(jnp.bfloat16)
                total = total + jnp.sum(w.reshape(STRIP // 8, 8, columns), axis=0)
            acc = acc + lax.dot_general(
                kv_held[chunk_rows(last, c), head_size:],
                low[0],
                (((0,), (0,)), ((), ())),
                preferred_element_type=jnp.float32,
            )
            return total, acc

        total, acc = lax.fori_loop(
            0,
            count,
            mix,
            (jnp.zeros((8, columns), jnp.float32), jnp.zeros((head_size, columns), jnp.float32)),
        )
        total = jnp.sum(total, axis=0, keepdims=True)
        mixed = (acc / total).astype(jnp.bfloat16)
        expected = jnp.sum(
            mixed.astype(jnp.float32) * c_columns[i].astype(jnp.float32), axis=0, keepdims=True
        )
        per_total = 1.0 / total
        for h in range(heads):
            mixed_out[here, h * head_size : (h + 1) * head_size] = mixed[
                :, h * block : (h + 1) * block
            ].T

        def back(c, q_acc):
            chunk = chunk_rows(last, c)
            prob_grad[...] = jnp.dot(
                kv_held[chunk, head_size:], c_columns[i], preferred_element_type=jnp.float32
            )
            for at in range(0, KEY_CHUNK, STRIP):
                strip = slice(at, at + STRIP)
                probability = scores[c, strip, :] * per_total
                low[0, strip, :] = probability.astype(jnp.bfloat16)
                low[1, strip, :] = (probability * (prob_grad[strip, :] - expected)).astype(
                    jnp.bfloat16
                )
            value_acc[chunk, :] += jnp.dot(low[0], c_rows[i], preferred_element_type=jnp.float32)
            key_acc[chunk, :] += jnp.dot(low[1], q_rows[i], preferred_element_type=jnp.float32)
            return q_acc + lax.dot_general(
                kv_held[chunk, :head_size],
                low[1],
                (((0,), (0,)), ((), ())),
                preferred_element_type=jnp.float32,
            )

        q_acc = lax.fori_loop(
            0, count, back, jnp.zeros((head_size, columns), jnp.float32)
        )
        q_grad = (q_acc * scale).astype(jnp.bfloat16)
        for h in range(heads):
            query_grad[here, h * head_size : (h + 1) * head_size] = q_grad[
                :, h * block : (h + 1) * block
            ].T
        return 0

    lax.fori_loop(0, 2 * own_blocks, one_block, 0)
    for _, core_of, out in sides:
        for j in range(blocks // 2):
            source = rows_at(true_block(core_of, j) + 1, block)
            part = slice(j * block, (j + 1) * block)
            out[part, :head_size] = (key_acc[source, :] * scale).astype(out.dtype)
            out[part, head_size:] = value_acc[source, :].astype(out.dtype)


def attention(meta, queries, cotangent, peer_both, kv_same, kv_other, head_size, docs, blocks):
    rows, width = queries.shape
    heads = width // head_size // 2
    length = kv_same.shape[0] + kv_other.shape[0]
    block = length // blocks
    columns = heads * block
    query_blocks = 2 * rows // block
    in_vmem = pl.BlockSpec(memory_space=pltpu.VMEM)
    most_chunks = 10
    visible = 9 * KEY_CHUNK
    return pl.pallas_call(
        functools.partial(
            attention_kernel, heads=heads, head_size=head_size, block=block, docs=docs, blocks=blocks
        ),
        out_shape=(
            jax.ShapeDtypeStruct((2 * rows, width // 2), jnp.bfloat16),
            jax.ShapeDtypeStruct((2 * rows, width // 2), jnp.bfloat16),
            jax.ShapeDtypeStruct(kv_same.shape, jnp.float32),
            jax.ShapeDtypeStruct(kv_other.shape, jnp.bfloat16),
        ),
        in_specs=[pl.BlockSpec(memory_space=pltpu.SMEM)] + [pl.BlockSpec(memory_space=pl.ANY)] * 5,
        out_specs=(in_vmem,) * 4,
        scratch_shapes=[
            pltpu.VMEM(queries.shape, jnp.bfloat16),
            pltpu.VMEM(cotangent.shape, jnp.bfloat16),
            pltpu.VMEM(peer_both.shape, jnp.bfloat16),
            pltpu.VMEM((block + length, 2 * head_size), jnp.bfloat16),
            pltpu.VMEM((block + length, head_size), jnp.float32),
            pltpu.VMEM((block + length, head_size), jnp.float32),
            pltpu.VMEM((most_chunks, KEY_CHUNK, columns), jnp.float32),
            pltpu.VMEM((KEY_CHUNK, columns), jnp.float32),
            pltpu.VMEM((2, KEY_CHUNK, columns), jnp.bfloat16),
            pltpu.VMEM((query_blocks, head_size, columns), jnp.bfloat16),
            pltpu.VMEM((query_blocks, head_size, columns), jnp.bfloat16),
            pltpu.VMEM((query_blocks, columns, head_size), jnp.bfloat16),
            pltpu.VMEM((query_blocks, columns, head_size), jnp.bfloat16),
            pltpu.SemaphoreType.DMA((5,)),
        ],
        compiler_params=pltpu.CompilerParams(vmem_limit_bytes=26 << 20),
        cost_estimate=pl.CostEstimate(
            flops=28 * rows * heads * visible * head_size,
            bytes_accessed=8 * rows * width + 8 * length * head_size,
            transcendentals=2 * rows * heads * visible,
        ),
        name="masked_attention",
    )(meta, queries, cotangent, peer_both, kv_same, kv_other)


def body(tokens, queries, cotangent, latent_key, latent_value, lengths, block_order):
    token_rows = tokens[0]
    rows_here, features = token_rows.shape
    head_size = latent_key.shape[1]
    docs, blocks = lengths.shape[1], block_order.shape[1]
    me = lax.axis_index(AXES)
    table = lax.dynamic_index_in_dim(jnp.asarray(block_table()), me, keepdims=False)
    before = np.arange(docs)[:, None] < np.arange(docs)[None, :]
    doc_starts = jnp.sum(jnp.where(before, lengths[0][:, None], 0), axis=0)
    meta = jnp.concatenate(
        [
            doc_starts.astype(jnp.int32),
            block_order[0],
            jnp.stack([lax.axis_index(CTX), lax.axis_index("core")]).astype(jnp.int32),
        ]
    )

    core = lax.axis_index("core")
    peer_both = swap_cores(
        jnp.concatenate(
            [
                lax.dynamic_slice_in_dim(a[0], (1 - core) * a.shape[2] // 2, a.shape[2] // 2, 1)
                for a in (queries, cotangent)
            ],
            axis=1,
        )
    )
    head_rows = latent_key.shape[0]
    latents = side_by_side(latent_key, latent_value)
    latents = gather_ring(jnp.concatenate(gather_ring(latents, 0), axis=0), 1)
    latents[0], peer_both, meta = lax.optimization_barrier((latents[0], peer_both, meta))
    sums = small(
        magnitudes_kernel,
        "magnitudes",
        jax.ShapeDtypeStruct((8, 2 * head_size), jnp.float32),
        *latents,
    )
    sums = sum(gather_ring(sums, 2))
    sums = sums + swap_cores(sums)
    weights = small(
        functools.partial(ternary_kernel, entries=features * head_size),
        "ternarize",
        jax.ShapeDtypeStruct((16 * head_rows, 2 * head_size), jnp.bfloat16),
        sums,
        *latents,
    )
    weights, shuffle_table = lax.optimization_barrier((weights, table))
    weight_parts = gather_ring(weights, 2)
    tokens_own, tokens_other = shuffle(shuffle_table, token_rows)
    other_parts = [swap_cores(part) for part in weight_parts]
    part_rows = weights.shape[0]
    projected = 0.0
    for i, (own, other) in enumerate(zip(weight_parts, other_parts)):
        cut = slice(i * part_rows, (i + 1) * part_rows)
        for rows, part in ((tokens_own, own), (tokens_other, other)):
            projected = projected + jnp.dot(
                rows[:, cut], part, preferred_element_type=jnp.float32
            )
    kv_here = projected.astype(jnp.bfloat16)
    groups = lax.axis_size(SAME_CORE_CTX)
    kv_same = lax.all_to_all(
        jnp.broadcast_to(kv_here[None], (groups,) + kv_here.shape).reshape(-1, 2 * head_size),
        SAME_CORE_CTX,
        split_axis=0,
        concat_axis=0,
        tiled=True,
    )
    kv_other = swap_cores(kv_same)
    tokens_peer = swap_cores(tokens_other)

    mixed, query_grad, same_terms, other_terms = attention(
        meta, queries[0], cotangent[0], peer_both, kv_same, kv_other, head_size, docs, blocks
    )
    same_terms, other_terms, tokens_peer = lax.optimization_barrier(
        (same_terms, other_terms, tokens_peer)
    )
    chip_terms = (same_terms + swap_cores(other_terms).astype(jnp.float32)).astype(jnp.bfloat16)
    terms = lax.all_to_all(chip_terms, SAME_CORE_CTX, split_axis=0, concat_axis=0, tiled=True)
    grads = jnp.sum(
        terms.reshape(groups, rows_here, 2 * head_size).astype(jnp.float32), axis=0
    ).astype(jnp.bfloat16)
    peer_grads = swap_cores(grads)

    arrived = sent_along_ring(
        weight_terms(grads, peer_grads, tokens_own, tokens_peer, 1, 3, jnp.bfloat16), 2
    )
    (summed,) = weight_terms(grads, peer_grads, tokens_own, tokens_peer, 0, 1, jnp.float32)
    summed = summed + sum(piece.astype(jnp.float32) for piece in arrived)
    token_grad = token_gradient(table, grads, weight_parts + other_parts)
    summed, token_grad = lax.optimization_barrier((summed, token_grad))
    from_peer = swap_cores(jnp.concatenate([mixed[rows_here:], query_grad[rows_here:]], axis=1))

    def both_halves(own, peers):
        return jnp.concatenate(
            [jnp.where(core == 0, own, peers), jnp.where(core == 0, peers, own)], axis=1
        )

    half_width = mixed.shape[1]
    mixed = both_halves(mixed[:rows_here], from_peer[:, :half_width])
    query_grad = both_halves(query_grad[:rows_here], from_peer[:, half_width:])
    summed, *pieces = jnp.split(summed, 4, axis=1)
    summed = summed + sum(piece.astype(jnp.float32) for piece in sent_along_ring(pieces, 1))
    summed, *pieces = jnp.split(summed, 4, axis=1)
    half_shape = jax.ShapeDtypeStruct((head_rows, head_size), jnp.float32)
    key_grad, value_grad = small(
        last_sum_kernel, "last_sum", (half_shape, half_shape), summed, *sent_along_ring(pieces, 0)
    )
    return (
        mixed[None],
        query_grad[None],
        token_grad[None],
        key_grad,
        value_grad,
    )


def solution(mesh):
    torus = Mesh(mesh.devices.reshape(SIZES), AXES)
    whole = CTX + DP
    in_specs = (
        P(DP, CTX, None),
        P(DP, CTX, None),
        P(DP, CTX, None),
        P(whole, None),
        P(whole, None),
        P(DP, None),
        P(DP, None),
    )
    out_specs = (
        P(DP, CTX, None),
        P(DP, CTX, None),
        P(DP, CTX, None),
        P(whole, None),
        P(whole, None),
    )
    return jax.shard_map(body, mesh=torus, in_specs=in_specs, out_specs=out_specs, check_vma=False)
```

profile of v0, /device:TPU:0, one launch (start us, length us, event | category | flops | bytes accessed | tf_op | source)
XLA Modules:
  0.0 208.4 jit_solution(7707449873366499328)
XLA Ops:
  2.2 3.2 %collective-permute-start.2 = (f32[128,256]{1,0:T(8,128)}, f32[128,256]{1,0:T(8,128)S(1)}, u32[]{:S(2)}, u32[]{:S(2)}) collective-permute-start(f32[128,256]{1,0:T(8,128)} %pair_latents.1), channel_id=1, source_target_pairs={{0,4},{1,5},{2,6},{3,7},{4,0},{5,1},{6,2},{7,3},{8,72},{9,73},{10,... | collective-permute-start | bytes 393224 | tf_op jit(solution)/shard_map/ppermute | solution.py:86
  10.5 2.4 %collective-permute-done = f32[128,256]{1,0:T(8,128)S(1)} collective-permute-done((f32[128,256]{1,0:T(8,128)}, f32[128,256]{1,0:T(8,128)S(1)}, u32[]{:S(2)}, u32[]{:S(2)}) %collective-permute-start) | collective-permute-done | bytes 131104 | tf_op jit(solution)/shard_map/ppermute | solution.py:86
  21.4 2.9 %collective-permute-done.4.refs_1_ = f32[512,256]{1,0:T(8,128)S(1)} collective-permute-done((f32[512,256]{1,0:T(8,128)S(1)}, f32[512,256]{1,0:T(8,128)S(1)}, u32[]{:S(2)}, u32[]{:S(2)}) %collective-permute-start.4) | collective-permute-done | bytes 524320 | tf_op jit(solution)/shard_map/ppermute | solution.py:86
  24.7 6.5 %collective-permute-done.6.refs_3_ = f32[512,256]{1,0:T(8,128)S(1)} collective-permute-done((f32[512,256]{1,0:T(8,128)S(1)}, f32[512,256]{1,0:T(8,128)S(1)}, u32[]{:S(2)}, u32[]{:S(2)}) %collective-permute-start.6) | collective-permute-done | bytes 524320 | tf_op jit(solution)/shard_map/ppermute | solution.py:86
  31.3 4.0 %collective-permute-start.9 = (f32[8,256]{1,0:T(8,128)S(1)}, f32[8,256]{1,0:T(8,128)S(1)}, u32[]{:S(2)}, u32[]{:S(2)}) collective-permute-start(f32[8,256]{1,0:T(8,128)S(1)} %magnitudes.1), channel_id=1, source_target_pairs={{0,16},{1,17},{2,18},{3,19},{4,20},{5,21},{6,22},{7,23},{8,12},{9,... | collective-permute-start | bytes 24584 | tf_op jit(solution)/shard_map/ppermute | solution.py:86
  43.2 3.1 %collective-permute-start.14 = (bf16[2048,256]{1,0:T(8,128)(2,1)S(1)}, bf16[2048,256]{1,0:T(8,128)(2,1)S(1)}, u32[]{:S(2)}, u32[]{:S(2)}) collective-permute-start(bf16[2048,256]{1,0:T(8,128)(2,1)S(1)} %ternarize.1.rest_0_), channel_id=1, source_target_pairs={{0,17},{1,0},{2,19},{3,2},{4,21},{5,4},{6,23},{7,6},{8,14},{9,15},... | collective-permute-start | bytes 3145736 | tf_op jit(solution)/shard_map/ppermute | solution.py:86
  47.2 3.4 %copy-done.1 = bf16[1,256,16384]{2,1,0:T(8,128)(2,1)S(1)} copy-done((bf16[1,256,16384]{2,1,0:T(8,128)(2,1)S(1)}, bf16[1,256,16384]{2,1,0:T(8,128)(2,1)}, u32[]{:S(2)}) %copy-start.1) | copy-done | bytes 8388632
  50.5 4.2 %shuffle_tokens.1 = (bf16[256,8192]{1,0:T(8,128)(2,1)S(1)}, bf16[256,8192]{1,0:T(8,128)(2,1)S(1)}) custom-call(s32[128]{0:T(128)S(1)} %fusion.14.table, bf16[256,16384]{1,0:T(8,128)(2,1)S(1)} %bitcast.28), custom_call_target="tpu_custom_call" | custom-call | bytes 16777216 | tf_op jit(solution)/shard_map/shuffle_tokens/pallas_call | solution.py:116
  54.9 15.5 %collective-permute-done.12.rest_1_ = bf16[2048,256]{1,0:T(8,128)(2,1)S(1)} collective-permute-done((bf16[2048,256]{1,0:T(8,128)(2,1)S(1)}, bf16[2048,256]{1,0:T(8,128)(2,1)S(1)}, u32[]{:S(2)}, u32[]{:S(2)}) %collective-permute-start.12) | collective-permute-done | bytes 1048608 | tf_op jit(solution)/shard_map/ppermute | solution.py:86
  77.1 20.2 %all_to_all.17 = bf16[8,256,256]{2,1,0:T(8,128)(2,1)S(1)} all-to-all(bf16[8,256,256]{2,1,0:T(8,128)(2,1)S(1)} %broadcast_in_dim.32), channel_id=1, replica_groups=mesh['y'=4,'zh'=2,'core'=2,'x'=4,'zl'=2] {'y','zh'}, dimensions={0} | all-to-all | bytes 2097152 | tf_op jit(solution)/shard_map/all_to_all | solution.py:624
  97.3 2.7 %collective-permute-done.18.kv_other = bf16[2048,256]{1,0:T(8,128)(2,1)S(1)} collective-permute-done((bf16[2048,256]{1,0:T(8,128)(2,1)S(1)}, bf16[2048,256]{1,0:T(8,128)(2,1)S(1)}, u32[]{:S(2)}, u32[]{:S(2)}) %collective-permute-start.18) | collective-permute-done | bytes 1048608 | tf_op jit(solution)/shard_map/ppermute | solution.py:63
  100.0 15.9 %masked_attention.1 = (bf16[512,512]{1,0:T(8,128)(2,1)S(1)}, bf16[512,512]{1,0:T(8,128)(2,1)S(1)}, f32[2048,256]{1,0:T(8,128)S(1)}, bf16[2048,256]{1,0:T(8,128)(2,1)S(1)}) custom-call(s32[42]{0:T(128)S(1)} %pad_add_fusion.meta, bf16[256,1024]{1,0:T(8,128)(2,1)S(1)} %bitcast.31, bf16[256,1024]{1,0:T(8,128)(2,1)S(1)} %bitcast.32, ...), custom_call_target="tpu_custom_call" | custom-call | flops 8455716864 | bytes 6291456 | tf_op jit(solution)/shard_map/masked_attention/pallas_call | solution.py:526
  116.1 2.5 %collective-permute-done.21 = bf16[2048,256]{1,0:T(8,128)(2,1)S(1)} collective-permute-done((bf16[2048,256]{1,0:T(8,128)(2,1)S(1)}, bf16[2048,256]{1,0:T(8,128)(2,1)S(1)}, u32[]{:S(2)}, u32[]{:S(2)}) %collective-permute-start.21) | collective-permute-done | bytes 1048608 | tf_op jit(solution)/shard_map/ppermute | solution.py:63
  118.9 25.9 %all_to_all.18 = bf16[8,256,256]{2,1,0:T(8,128)(2,1)S(1)} all-to-all(bf16[8,256,256]{2,1,0:T(8,128)(2,1)S(1)} %bitcast.34), channel_id=1, replica_groups=mesh['y'=4,'zh'=2,'core'=2,'x'=4,'zl'=2] {'y','zh'}, dimensions={0} | all-to-all | bytes 2097152 | tf_op jit(solution)/shard_map/all_to_all | solution.py:641
  147.0 6.4 %weight_terms.3 = (bf16[256,2048]{1,0:T(8,128)(2,1)}, bf16[256,2048]{1,0:T(8,128)(2,1)}, bf16[256,2048]{1,0:T(8,128)(2,1)}) custom-call(bf16[256,256]{1,0:T(8,128)(2,1)} %copy-done.11, bf16[256,256]{1,0:T(8,128)(2,1)} %copy-done.17, bf16[256,8192]{1,0:T(8,128)(2,1)} %copy-done, bf16[256,8192]{1,0:T(8,128)(2,1)} %copy-done.8), custom_call_target="tpu_custom_call" | custom-call | flops 1610612736 | bytes 9437184 | tf_op jit(solution)/shard_map/weight_terms/pallas_call | solution.py:183
  158.1 2.6 %collective-permute-start.19 = (bf16[256,1024]{1,0:T(8,128)(2,1)S(1)}, bf16[256,1024]{1,0:T(8,128)(2,1)S(1)}, u32[]{:S(2)}, u32[]{:S(2)}) collective-permute-start(bf16[256,1024]{1,0:T(8,128)(2,1)S(1)} %pad_maximum_fusion.2), channel_id=1, source_target_pairs={{0,8},{1,9},{2,10},{3,11},{4,12},{5,13},{6,14},{7,15},{8,0},{9,1},... | collective-permute-start | bytes 1572872 | tf_op jit(solution)/shard_map/ppermute | solution.py:63
  160.7 11.2 %token_gradient.1 = bf16[256,16384]{1,0:T(8,128)(2,1)} custom-call(s32[128]{0:T(128)} %copy-done.5, bf16[256,256]{1,0:T(8,128)(2,1)} %copy-done.11, bf16[2048,256]{1,0:T(8,128)(2,1)} %copy-done.2, bf16[2048,256]{1,0:T(8,128)(2,1)} %copy-done.12, bf16[2048,256]{1,0:T(8,128)(2,1)} %copy-done.13, bf16[2048,256]{1,0:T(8,128)(2,1)} %copy-done.15, ...), custom_call_target="tpu_custom_call" | custom-call | flops 2147483648 | bytes 16777216 | tf_op jit(solution)/shard_map/token_gradient/pallas_call | solution.py:323
  171.9 3.4 %weight_terms.2 = f32[256,2048]{1,0:T(8,128)} custom-call(bf16[256,256]{1,0:T(8,128)(2,1)} %copy-done.11, bf16[256,256]{1,0:T(8,128)(2,1)} %copy-done.17, bf16[256,8192]{1,0:T(8,128)(2,1)} %copy-done, bf16[256,8192]{1,0:T(8,128)(2,1)} %copy-done.8), custom_call_target="tpu_custom_call" | custom-call | flops 536870912 | bytes 3145728 | tf_op jit(solution)/shard_map/weight_terms/pallas_call | solution.py:183
  175.3 6.0 %collective-permute-done.24 = bf16[256,2048]{1,0:T(8,128)(2,1)S(1)} collective-permute-done((bf16[256,2048]{1,0:T(8,128)(2,1)}, bf16[256,2048]{1,0:T(8,128)(2,1)S(1)}, u32[]{:S(2)}, u32[]{:S(2)}) %collective-permute-start.24) | collective-permute-done | bytes 1048608 | tf_op jit(solution)/shard_map/ppermute | solution.py:92
  181.3 2.5 %add_add_fusion = f32[256,2048]{1,0:T(8,128)S(1)} fusion(f32[256,2048]{1,0:T(8,128)} %weight_terms.2, bf16[256,2048]{1,0:T(8,128)(2,1)S(1)} %collective-permute-done.25, bf16[256,2048]{1,0:T(8,128)(2,1)S(1)} %collective-permute-done.24, bf16[256,2048]{1,0:T(8,128)(2,1)} %collective-permute-done.23), kind=kLoop, calls=%fused_computation | loop fusion | flops 3145728 | bytes 7340032 | tf_op jit(solution)/shard_map/add | solution.py:651
  185.9 2.8 %collective-permute-start.26 = (bf16[256,512]{1,0:T(8,128)(2,1)S(1)}, bf16[256,512]{1,0:T(8,128)(2,1)S(1)}, u32[]{:S(2)}, u32[]{:S(2)}) collective-permute-start(bf16[256,512]{1,0:T(8,128)(2,1)S(1)} %get-tuple-element.49), channel_id=1, source_target_pairs={{0,96},{1,97},{2,98},{3,99},{4,100},{5,101},{6,102},{7,103},{8,25}... | collective-permute-start | bytes 786440 | tf_op jit(solution)/shard_map/ppermute | solution.py:92
  192.0 2.7 %collective-permute-done.27 = bf16[256,512]{1,0:T(8,128)(2,1)S(1)} collective-permute-done((bf16[256,512]{1,0:T(8,128)(2,1)S(1)}, bf16[256,512]{1,0:T(8,128)(2,1)S(1)}, u32[]{:S(2)}, u32[]{:S(2)}) %collective-permute-start.27) | collective-permute-done | bytes 262176 | tf_op jit(solution)/shard_map/ppermute | solution.py:92
  194.9 5.1 %collective-permute-start.29 = (bf16[256,128]{1,0:T(8,128)(2,1)S(1)}, bf16[256,128]{1,0:T(8,128)(2,1)S(1)}, u32[]{:S(2)}, u32[]{:S(2)}) collective-permute-start(bf16[256,128]{1,0:T(8,128)(2,1)S(1)} %get-tuple-element.60), channel_id=1, source_target_pairs={{0,6},{1,7},{2,0},{3,1},{4,2},{5,3},{6,4},{7,5},{8,104},{9,105},{1... | collective-permute-start | bytes 196616 | tf_op jit(solution)/shard_map/ppermute | solution.py:92
  200.0 4.7 %collective-permute-start.31 = (bf16[256,128]{1,0:T(8,128)(2,1)S(1)}, bf16[256,128]{1,0:T(8,128)(2,1)S(1)}, u32[]{:S(2)}, u32[]{:S(2)}) collective-permute-start(bf16[256,128]{1,0:T(8,128)(2,1)S(1)} %get-tuple-element.58), channel_id=1, source_target_pairs={{0,4},{1,5},{2,6},{3,7},{4,0},{5,1},{6,2},{7,3},{8,72},{9,73},{10,... | collective-permute-start | bytes 196616 | tf_op jit(solution)/shard_map/ppermute | solution.py:92
  (118 shorter events, 47.7 us)
Async XLA Ops:
  2.2 6.8 %collective-permute-start.2 = (f32[128,256]{1,0:T(8,128)}, f32[128,256]{1,0:T(8,128)S(1)}, u32[]{:S(2)}, u32[]{:S(2)}) collective-permute-start(f32[128,256]{1,0:T(8,128)} %pair_latents.1), channel_id=1, source_target_pairs={{0,4},{1,5},{2,6},{3,7},{4,0},{5,1},{6,2},{7,3},{8,72},{9,73},{10,... | collective-permute-start | bytes 393224 | tf_op jit(solution)/shard_map/ppermute | solution.py:86
  5.4 5.2 %collective-permute-start.1 = (f32[128,256]{1,0:T(8,128)}, f32[128,256]{1,0:T(8,128)S(1)}, u32[]{:S(2)}, u32[]{:S(2)}) collective-permute-start(f32[128,256]{1,0:T(8,128)} %pair_latents.1), channel_id=1, source_target_pairs={{0,6},{1,7},{2,0},{3,1},{4,2},{5,3},{6,4},{7,5},{8,104},{9,105},{1... | collective-permute-start | bytes 393224 | tf_op jit(solution)/shard_map/ppermute | solution.py:86
  6.5 6.4 %collective-permute-start = (f32[128,256]{1,0:T(8,128)}, f32[128,256]{1,0:T(8,128)S(1)}, u32[]{:S(2)}, u32[]{:S(2)}) collective-permute-start(f32[128,256]{1,0:T(8,128)} %pair_latents.1), channel_id=1, source_target_pairs={{0,2},{1,3},{2,4},{3,5},{4,6},{5,7},{6,0},{7,1},{8,40},{9,41},{10,... | collective-permute-start | bytes 393224 | tf_op jit(solution)/shard_map/ppermute | solution.py:86
  8.8 11.9 %collective-permute-start.3 = (bf16[256,1024]{1,0:T(8,128)(2,1)S(1)}, bf16[256,1024]{1,0:T(8,128)(2,1)S(1)}, u32[]{:S(2)}, u32[]{:S(2)}) collective-permute-start(bf16[256,1024]{1,0:T(8,128)(2,1)S(1)} %pad_maximum_fusion.1), channel_id=1, source_target_pairs={{0,8},{1,9},{2,10},{3,11},{4,12},{5,13},{6,14},{7,15},{8,0},{9,1},... | collective-permute-start | bytes 1572872 | tf_op jit(solution)/shard_map/ppermute | solution.py:63
  13.8 10.5 %collective-permute-start.4 = (f32[512,256]{1,0:T(8,128)S(1)}, f32[512,256]{1,0:T(8,128)S(1)}, u32[]{:S(2)}, u32[]{:S(2)}) collective-permute-start(f32[512,256]{1,0:T(8,128)S(1)} %pad_maximum_fusion.refs_0_), channel_id=1, source_target_pairs={{0,32},{1,33},{2,34},{3,35},{4,36},{5,37},{6,38},{7,39},{8,9},{9,2... | collective-permute-start | bytes 1572872 | tf_op jit(solution)/shard_map/ppermute | solution.py:86
  15.5 9.2 %collective-permute-start.5 = (f32[512,256]{1,0:T(8,128)S(1)}, f32[512,256]{1,0:T(8,128)S(1)}, u32[]{:S(2)}, u32[]{:S(2)}) collective-permute-start(f32[512,256]{1,0:T(8,128)S(1)} %pad_maximum_fusion.refs_0_), channel_id=1, source_target_pairs={{0,96},{1,97},{2,98},{3,99},{4,100},{5,101},{6,102},{7,103},{8,25}... | collective-permute-start | bytes 1572872 | tf_op jit(solution)/shard_map/ppermute | solution.py:86
  17.1 14.0 %collective-permute-start.6 = (f32[512,256]{1,0:T(8,128)S(1)}, f32[512,256]{1,0:T(8,128)S(1)}, u32[]{:S(2)}, u32[]{:S(2)}) collective-permute-start(f32[512,256]{1,0:T(8,128)S(1)} %pad_maximum_fusion.refs_0_), channel_id=1, source_target_pairs={{0,64},{1,65},{2,66},{3,67},{4,68},{5,69},{6,70},{7,71},{8,24},{9,... | collective-permute-start | bytes 1572872 | tf_op jit(solution)/shard_map/ppermute | solution.py:86
  31.3 6.0 %collective-permute-start.9 = (f32[8,256]{1,0:T(8,128)S(1)}, f32[8,256]{1,0:T(8,128)S(1)}, u32[]{:S(2)}, u32[]{:S(2)}) collective-permute-start(f32[8,256]{1,0:T(8,128)S(1)} %magnitudes.1), channel_id=1, source_target_pairs={{0,16},{1,17},{2,18},{3,19},{4,20},{5,21},{6,22},{7,23},{8,12},{9,... | collective-permute-start | bytes 24584 | tf_op jit(solution)/shard_map/ppermute | solution.py:86
  36.0 4.9 %collective-permute-start.7 = (f32[8,256]{1,0:T(8,128)S(1)}, f32[8,256]{1,0:T(8,128)S(1)}, u32[]{:S(2)}, u32[]{:S(2)}) collective-permute-start(f32[8,256]{1,0:T(8,128)S(1)} %magnitudes.1), channel_id=1, source_target_pairs={{0,1},{1,16},{2,3},{3,18},{4,5},{5,20},{6,7},{7,22},{8,10},{9,11},... | collective-permute-start | bytes 24584 | tf_op jit(solution)/shard_map/ppermute | solution.py:86
  43.1 27.3 %collective-permute-start.12 = (bf16[2048,256]{1,0:T(8,128)(2,1)S(1)}, bf16[2048,256]{1,0:T(8,128)(2,1)S(1)}, u32[]{:S(2)}, u32[]{:S(2)}) collective-permute-start(bf16[2048,256]{1,0:T(8,128)(2,1)S(1)} %ternarize.1.rest_0_), channel_id=1, source_target_pairs={{0,1},{1,16},{2,3},{3,18},{4,5},{5,20},{6,7},{7,22},{8,10},{9,11},... | collective-permute-start | bytes 3145736 | tf_op jit(solution)/shard_map/ppermute | solution.py:86
  43.2 27.2 %collective-permute-start.14 = (bf16[2048,256]{1,0:T(8,128)(2,1)S(1)}, bf16[2048,256]{1,0:T(8,128)(2,1)S(1)}, u32[]{:S(2)}, u32[]{:S(2)}) collective-permute-start(bf16[2048,256]{1,0:T(8,128)(2,1)S(1)} %ternarize.1.rest_0_), channel_id=1, source_target_pairs={{0,17},{1,0},{2,19},{3,2},{4,21},{5,4},{6,23},{7,6},{8,14},{9,15},... | collective-permute-start | bytes 3145736 | tf_op jit(solution)/shard_map/ppermute | solution.py:86
  46.4 24.5 %collective-permute-start.11 = (bf16[2048,256]{1,0:T(8,128)(2,1)S(1)}, bf16[2048,256]{1,0:T(8,128)(2,1)S(1)}, u32[]{:S(2)}, u32[]{:S(2)}) collective-permute-start(bf16[2048,256]{1,0:T(8,128)(2,1)S(1)} %ternarize.1.rest_0_), channel_id=1, source_target_pairs={{0,8},{1,9},{2,10},{3,11},{4,12},{5,13},{6,14},{7,15},{8,0},{9,1},... | collective-permute-start | bytes 3145736 | tf_op jit(solution)/shard_map/ppermute | solution.py:63
  46.4 25.0 %collective-permute-start.16 = (bf16[2048,256]{1,0:T(8,128)(2,1)S(1)}, bf16[2048,256]{1,0:T(8,128)(2,1)S(1)}, u32[]{:S(2)}, u32[]{:S(2)}) collective-permute-start(bf16[2048,256]{1,0:T(8,128)(2,1)S(1)} %ternarize.1.rest_0_), channel_id=1, source_target_pairs={{0,16},{1,17},{2,18},{3,19},{4,20},{5,21},{6,22},{7,23},{8,12},{9,... | collective-permute-start | bytes 3145736 | tf_op jit(solution)/shard_map/ppermute | solution.py:86
  54.8 61.1 %collective-permute-start.20 = (bf16[256,8192]{1,0:T(8,128)(2,1)S(1)}, bf16[256,8192]{1,0:T(8,128)(2,1)S(1)}, u32[]{:S(2)}, u32[]{:S(2)}) collective-permute-start(bf16[256,8192]{1,0:T(8,128)(2,1)S(1)} %get-tuple-element.32), channel_id=1, source_target_pairs={{0,8},{1,9},{2,10},{3,11},{4,12},{5,13},{6,14},{7,15},{8,0},{9,1},... | collective-permute-start | bytes 12582920 | tf_op jit(solution)/shard_map/ppermute | solution.py:63
  153.4 21.8 %collective-permute-start.25 = (bf16[256,2048]{1,0:T(8,128)(2,1)}, bf16[256,2048]{1,0:T(8,128)(2,1)S(1)}, u32[]{:S(2)}, u32[]{:S(2)}) collective-permute-start(bf16[256,2048]{1,0:T(8,128)(2,1)} %get-tuple-element.42), channel_id=1, source_target_pairs={{0,16},{1,17},{2,18},{3,19},{4,20},{5,21},{6,22},{7,23},{8,12},{9,... | collective-permute-start | bytes 3145736 | tf_op jit(solution)/shard_map/ppermute | solution.py:92
  154.7 26.5 %collective-permute-start.24 = (bf16[256,2048]{1,0:T(8,128)(2,1)}, bf16[256,2048]{1,0:T(8,128)(2,1)S(1)}, u32[]{:S(2)}, u32[]{:S(2)}) collective-permute-start(bf16[256,2048]{1,0:T(8,128)(2,1)} %get-tuple-element.41), channel_id=1, source_target_pairs={{0,1},{1,16},{2,3},{3,18},{4,5},{5,20},{6,7},{7,22},{8,10},{9,11},... | collective-permute-start | bytes 3145736 | tf_op jit(solution)/shard_map/ppermute | solution.py:92
  156.1 25.2 %collective-permute-start.23 = (bf16[256,2048]{1,0:T(8,128)(2,1)}, bf16[256,2048]{1,0:T(8,128)(2,1)}, u32[]{:S(2)}, u32[]{:S(2)}) collective-permute-start(bf16[256,2048]{1,0:T(8,128)(2,1)} %get-tuple-element.40), channel_id=1, source_target_pairs={{0,17},{1,0},{2,19},{3,2},{4,21},{5,4},{6,23},{7,6},{8,14},{9,15},... | collective-permute-start | bytes 3145736 | tf_op jit(solution)/shard_map/ppermute | solution.py:92
  158.1 30.7 %collective-permute-start.19 = (bf16[256,1024]{1,0:T(8,128)(2,1)S(1)}, bf16[256,1024]{1,0:T(8,128)(2,1)S(1)}, u32[]{:S(2)}, u32[]{:S(2)}) collective-permute-start(bf16[256,1024]{1,0:T(8,128)(2,1)S(1)} %pad_maximum_fusion.2), channel_id=1, source_target_pairs={{0,8},{1,9},{2,10},{3,11},{4,12},{5,13},{6,14},{7,15},{8,0},{9,1},... | collective-permute-start | bytes 1572872 | tf_op jit(solution)/shard_map/ppermute | solution.py:63
  184.0 8.1 %collective-permute-start.28 = (bf16[256,512]{1,0:T(8,128)(2,1)S(1)}, bf16[256,512]{1,0:T(8,128)(2,1)S(1)}, u32[]{:S(2)}, u32[]{:S(2)}) collective-permute-start(bf16[256,512]{1,0:T(8,128)(2,1)S(1)} %get-tuple-element.50), channel_id=1, source_target_pairs={{0,64},{1,65},{2,66},{3,67},{4,68},{5,69},{6,70},{7,71},{8,24},{9,... | collective-permute-start | bytes 786440 | tf_op jit(solution)/shard_map/ppermute | solution.py:92
  185.5 9.2 %collective-permute-start.27 = (bf16[256,512]{1,0:T(8,128)(2,1)S(1)}, bf16[256,512]{1,0:T(8,128)(2,1)S(1)}, u32[]{:S(2)}, u32[]{:S(2)}) collective-permute-start(bf16[256,512]{1,0:T(8,128)(2,1)S(1)} %get-tuple-element.51), channel_id=1, source_target_pairs={{0,32},{1,33},{2,34},{3,35},{4,36},{5,37},{6,38},{7,39},{8,9},{9,2... | collective-permute-start | bytes 786440 | tf_op jit(solution)/shard_map/ppermute | solution.py:92
  185.9 8.8 %collective-permute-start.26 = (bf16[256,512]{1,0:T(8,128)(2,1)S(1)}, bf16[256,512]{1,0:T(8,128)(2,1)S(1)}, u32[]{:S(2)}, u32[]{:S(2)}) collective-permute-start(bf16[256,512]{1,0:T(8,128)(2,1)S(1)} %get-tuple-element.49), channel_id=1, source_target_pairs={{0,96},{1,97},{2,98},{3,99},{4,100},{5,101},{6,102},{7,103},{8,25}... | collective-permute-start | bytes 786440 | tf_op jit(solution)/shard_map/ppermute | solution.py:92
  194.9 10.7 %collective-permute-start.29 = (bf16[256,128]{1,0:T(8,128)(2,1)S(1)}, bf16[256,128]{1,0:T(8,128)(2,1)S(1)}, u32[]{:S(2)}, u32[]{:S(2)}) collective-permute-start(bf16[256,128]{1,0:T(8,128)(2,1)S(1)} %get-tuple-element.60), channel_id=1, source_target_pairs={{0,6},{1,7},{2,0},{3,1},{4,2},{5,3},{6,4},{7,5},{8,104},{9,105},{1... | collective-permute-start | bytes 196616 | tf_op jit(solution)/shard_map/ppermute | solution.py:92
  200.0 5.6 %collective-permute-start.30 = (bf16[256,128]{1,0:T(8,128)(2,1)S(1)}, bf16[256,128]{1,0:T(8,128)(2,1)S(1)}, u32[]{:S(2)}, u32[]{:S(2)}) collective-permute-start(bf16[256,128]{1,0:T(8,128)(2,1)S(1)} %get-tuple-element.59), channel_id=1, source_target_pairs={{0,2},{1,3},{2,4},{3,5},{4,6},{5,7},{6,0},{7,1},{8,40},{9,41},{10,... | collective-permute-start | bytes 196616 | tf_op jit(solution)/shard_map/ppermute | solution.py:92
  200.0 7.6 %collective-permute-start.31 = (bf16[256,128]{1,0:T(8,128)(2,1)S(1)}, bf16[256,128]{1,0:T(8,128)(2,1)S(1)}, u32[]{:S(2)}, u32[]{:S(2)}) collective-permute-start(bf16[256,128]{1,0:T(8,128)(2,1)S(1)} %get-tuple-element.58), channel_id=1, source_target_pairs={{0,4},{1,5},{2,6},{3,7},{4,0},{5,1},{6,2},{7,3},{8,72},{9,73},{10,... | collective-permute-start | bytes 196616 | tf_op jit(solution)/shard_map/ppermute | solution.py:92
  (26 other events, 206.8 us)
where the time goes:
time: 210 us; the launch traced here: 208 us
  waiting for transfers between devices  54.7 us (26%)
  blocking collectives  46.1 us (22%)
  Pallas kernels  44.6 us (21%)
  starting transfers between devices  43.4 us (21%)
  local copies, waits for them, and re-layouts  7.63 us (4%)
  other arithmetic  7.49 us (4%)
  matrix products  3.49 us (2%)
    ppermute x12, waiting for transfers between devices, gather_ring(): lax.ppermute(value, AXES, along_ring(phase, -offset))  32.9 us
    all_to_all x1, blocking collectives, body(): lax.all_to_all(chip_terms, SAME_CORE_CTX, split_axis=0, concat_axis=0, ti...  25.9 us
    ppermute x12, starting transfers between devices, gather_ring(): lax.ppermute(value, AXES, along_ring(phase, -offset))  20.5 us
    all_to_all x1, blocking collectives, body(): lax.all_to_all(jnp.broadcast_to(kv_here[None], (groups,) + kv_here.shape)...  20.2 us
    ppermute x9, starting transfers between devices, sent_along_ring(): lax.ppermute(piece.astype(jnp.bfloat16), AXES, along_ring(phase, offset))  19.1 us
    pallas_call x1, Pallas kernels, attention(): pl.pallas_call(functools.partial(attention_kernel, heads=heads, head_size...  15.9 us
    ppermute x9, waiting for transfers between devices, sent_along_ring(): lax.ppermute(piece.astype(jnp.bfloat16), AXES, along_ring(phase, offset))  13.1 us
    pallas_call x1, Pallas kernels, token_gradient(): pl.pallas_call(functools.partial(token_grad_kernel, count=len(weights)),...  11.2 us
  transfers between devices with their start and end apart: 32, of which 19 were waited for; matrix products, arithmetic and copies ran while one was open for 6% of the time, Pallas kernels for 17%

commit v1 on v0

--- a/solution.py
+++ b/solution.py
@@ -87,10 +87,10 @@
     ]
 
 
-def sent_along_ring(pieces, phase):
+def sent_along_ring(pieces, phase, offsets=OFFSETS[1:]):
     return [
         lax.ppermute(piece.astype(jnp.bfloat16), AXES, along_ring(phase, offset))
-        for piece, offset in zip(pieces, OFFSETS[1:])
+        for piece, offset in zip(pieces, offsets)
     ]
 
 
@@ -644,9 +644,13 @@
     ).astype(jnp.bfloat16)
     peer_grads = swap_cores(grads)
 
+    (opposite,) = sent_along_ring(
+        weight_terms(grads, peer_grads, tokens_own, tokens_peer, 3, 1, jnp.bfloat16), 2, OFFSETS[3:]
+    )
     arrived = sent_along_ring(
-        weight_terms(grads, peer_grads, tokens_own, tokens_peer, 1, 3, jnp.bfloat16), 2
-    )
+        weight_terms(grads, peer_grads, tokens_own, tokens_peer, 1, 2, jnp.bfloat16), 2, OFFSETS[1:3]
+    )
+    arrived.append(opposite)
     (summed,) = weight_terms(grads, peer_grads, tokens_own, tokens_peer, 0, 1, jnp.float32)
     summed = summed + sum(piece.astype(jnp.float32) for piece in arrived)
     token_grad = token_gradient(table, grads, weight_parts + other_parts)

time: 210 us -> 208 us (level)
  starting transfers between devices: 43.4 us -> 33.6 us
  blocking collectives: 46.1 us -> 52.3 us
  Pallas kernels: 44.6 us -> 48.1 us
    ppermute x9, starting transfers between devices: 19.1 us -> 11.6 us  [sent_along_ring(): lax.ppermute(piece.astype(jnp.bfloat16), AXES, along_ring(phase, offset))]
    all_to_all x1, blocking collectives: 25.9 us -> 32.1 us  [body(): lax.all_to_all(chip_terms, SAME_CORE_CTX, split_axis=0, concat_axis=0, ti...]
    ppermute x11, starting transfers between devices: 3.76 us -> 1.47 us  [swap_cores(): return lax.ppermute(value, AXES, moved(to_other_core))]
    pallas_call x2 -> x3, Pallas kernels: 9.86 us -> 11.6 us  [weight_terms(): pl.pallas_call(functools.partial(weight_terms_kernel, first=first * width...]
  transfers between devices with their start and end apart: 32 -> 32, of which waited for: 19 -> 21; matrix products, arithmetic and copies ran while one was open for 6% -> 6% of each run, Pallas kernels for 17% -> 20%
where the time goes in v1:
time: 208 us
  waiting for transfers between devices  54.7 us (26%)
  blocking collectives  52.3 us (25%)
  Pallas kernels  48.1 us (23%)
  starting transfers between devices  33.6 us (16%)
  local copies, waits for them, and re-layouts  7.63 us (4%)
  other arithmetic  7.49 us (4%)
  matrix products  3.49 us (2%)
    ppermute x12, waiting for transfers between devices, gather_ring(): lax.ppermute(value, AXES, along_ring(phase, -offset))  32.9 us
    all_to_all x1, blocking collectives, body(): lax.all_to_all(chip_terms, SAME_CORE_CTX, split_axis=0, concat_axis=0, ti...  32.1 us
    ppermute x12, starting transfers between devices, gather_ring(): lax.ppermute(value, AXES, along_ring(phase, -offset))  20.5 us
    all_to_all x1, blocking collectives, body(): lax.all_to_all(jnp.broadcast_to(kv_here[None], (groups,) + kv_here.shape)...  20.2 us
    pallas_call x1, Pallas kernels, attention(): pl.pallas_call(functools.partial(attention_kernel, heads=heads, head_size...  17.7 us
    ppermute x9, waiting for transfers between devices, sent_along_ring(): lax.ppermute(piece.astype(jnp.bfloat16), AXES, along_ring(phase, offset))  13.1 us
    ppermute x9, starting transfers between devices, sent_along_ring(): lax.ppermute(piece.astype(jnp.bfloat16), AXES, along_ring(phase, offset))  11.6 us
    pallas_call x3, Pallas kernels, weight_terms(): pl.pallas_call(functools.partial(weight_terms_kernel, first=first * width...  11.6 us
  transfers between devices with their start and end apart: 32, of which 21 were waited for; matrix products, arithmetic and copies ran while one was open for 6% of the time, Pallas kernels for 20%

profile of v1, /device:TPU:0, one launch (start us, length us, event | category | flops | bytes accessed | tf_op | source)
XLA Modules:
  0.0 208.4 jit_solution(8424732524992674716)
XLA Ops:
  2.2 3.2 %collective-permute-start.2 = (f32[128,256]{1,0:T(8,128)}, f32[128,256]{1,0:T(8,128)S(1)}, u32[]{:S(2)}, u32[]{:S(2)}) collective-permute-start(f32[128,256]{1,0:T(8,128)} %pair_latents.1), channel_id=1, source_target_pairs={{0,4},{1,5},{2,6},{3,7},{4,0},{5,1},{6,2},{7,3},{8,72},{9,73},{10,... | collective-permute-start | bytes 393224 | tf_op jit(solution)/shard_map/ppermute | solution.py:86
  10.5 2.4 %collective-permute-done = f32[128,256]{1,0:T(8,128)S(1)} collective-permute-done((f32[128,256]{1,0:T(8,128)}, f32[128,256]{1,0:T(8,128)S(1)}, u32[]{:S(2)}, u32[]{:S(2)}) %collective-permute-start) | collective-permute-done | bytes 131104 | tf_op jit(solution)/shard_map/ppermute | solution.py:86
  21.4 2.9 %collective-permute-done.4.refs_1_ = f32[512,256]{1,0:T(8,128)S(1)} collective-permute-done((f32[512,256]{1,0:T(8,128)S(1)}, f32[512,256]{1,0:T(8,128)S(1)}, u32[]{:S(2)}, u32[]{:S(2)}) %collective-permute-start.4) | collective-permute-done | bytes 524320 | tf_op jit(solution)/shard_map/ppermute | solution.py:86
  24.7 6.5 %collective-permute-done.6.refs_3_ = f32[512,256]{1,0:T(8,128)S(1)} collective-permute-done((f32[512,256]{1,0:T(8,128)S(1)}, f32[512,256]{1,0:T(8,128)S(1)}, u32[]{:S(2)}, u32[]{:S(2)}) %collective-permute-start.6) | collective-permute-done | bytes 524320 | tf_op jit(solution)/shard_map/ppermute | solution.py:86
  31.3 4.0 %collective-permute-start.9 = (f32[8,256]{1,0:T(8,128)S(1)}, f32[8,256]{1,0:T(8,128)S(1)}, u32[]{:S(2)}, u32[]{:S(2)}) collective-permute-start(f32[8,256]{1,0:T(8,128)S(1)} %magnitudes.1), channel_id=1, source_target_pairs={{0,16},{1,17},{2,18},{3,19},{4,20},{5,21},{6,22},{7,23},{8,12},{9,... | collective-permute-start | bytes 24584 | tf_op jit(solution)/shard_map/ppermute | solution.py:86
  43.2 3.1 %collective-permute-start.14 = (bf16[2048,256]{1,0:T(8,128)(2,1)S(1)}, bf16[2048,256]{1,0:T(8,128)(2,1)S(1)}, u32[]{:S(2)}, u32[]{:S(2)}) collective-permute-start(bf16[2048,256]{1,0:T(8,128)(2,1)S(1)} %ternarize.1.rest_0_), channel_id=1, source_target_pairs={{0,17},{1,0},{2,19},{3,2},{4,21},{5,4},{6,23},{7,6},{8,14},{9,15},... | collective-permute-start | bytes 3145736 | tf_op jit(solution)/shard_map/ppermute | solution.py:86
  47.2 3.4 %copy-done.1 = bf16[1,256,16384]{2,1,0:T(8,128)(2,1)S(1)} copy-done((bf16[1,256,16384]{2,1,0:T(8,128)(2,1)S(1)}, bf16[1,256,16384]{2,1,0:T(8,128)(2,1)}, u32[]{:S(2)}) %copy-start.1) | copy-done | bytes 8388632
  50.5 4.2 %shuffle_tokens.1 = (bf16[256,8192]{1,0:T(8,128)(2,1)S(1)}, bf16[256,8192]{1,0:T(8,128)(2,1)S(1)}) custom-call(s32[128]{0:T(128)S(1)} %fusion.14.table, bf16[256,16384]{1,0:T(8,128)(2,1)S(1)} %bitcast.28), custom_call_target="tpu_custom_call" | custom-call | bytes 16777216 | tf_op jit(solution)/shard_map/shuffle_tokens/pallas_call | solution.py:116
  54.9 15.5 %collective-permute-done.12.rest_1_ = bf16[2048,256]{1,0:T(8,128)(2,1)S(1)} collective-permute-done((bf16[2048,256]{1,0:T(8,128)(2,1)S(1)}, bf16[2048,256]{1,0:T(8,128)(2,1)S(1)}, u32[]{:S(2)}, u32[]{:S(2)}) %collective-permute-start.12) | collective-permute-done | bytes 1048608 | tf_op jit(solution)/shard_map/ppermute | solution.py:86
  77.1 20.2 %all_to_all.17 = bf16[8,256,256]{2,1,0:T(8,128)(2,1)S(1)} all-to-all(bf16[8,256,256]{2,1,0:T(8,128)(2,1)S(1)} %broadcast_in_dim.32), channel_id=1, replica_groups=mesh['y'=4,'zh'=2,'core'=2,'x'=4,'zl'=2] {'y','zh'}, dimensions={0} | all-to-all | bytes 2097152 | tf_op jit(solution)/shard_map/all_to_all | solution.py:624
  97.3 2.7 %collective-permute-done.18.kv_other = bf16[2048,256]{1,0:T(8,128)(2,1)S(1)} collective-permute-done((bf16[2048,256]{1,0:T(8,128)(2,1)S(1)}, bf16[2048,256]{1,0:T(8,128)(2,1)S(1)}, u32[]{:S(2)}, u32[]{:S(2)}) %collective-permute-start.18) | collective-permute-done | bytes 1048608 | tf_op jit(solution)/shard_map/ppermute | solution.py:63
  100.0 17.7 %masked_attention.1 = (bf16[512,512]{1,0:T(8,128)(2,1)S(1)}, bf16[512,512]{1,0:T(8,128)(2,1)S(1)}, f32[2048,256]{1,0:T(8,128)S(1)}, bf16[2048,256]{1,0:T(8,128)(2,1)S(1)}) custom-call(s32[42]{0:T(128)S(1)} %pad_add_fusion.meta, bf16[256,1024]{1,0:T(8,128)(2,1)S(1)} %bitcast.31, bf16[256,1024]{1,0:T(8,128)(2,1)S(1)} %bitcast.32, ...), custom_call_target="tpu_custom_call" | custom-call | flops 8455716864 | bytes 6291456 | tf_op jit(solution)/shard_map/masked_attention/pallas_call | solution.py:526
  117.9 2.5 %collective-permute-done.21 = bf16[2048,256]{1,0:T(8,128)(2,1)S(1)} collective-permute-done((bf16[2048,256]{1,0:T(8,128)(2,1)S(1)}, bf16[2048,256]{1,0:T(8,128)(2,1)S(1)}, u32[]{:S(2)}, u32[]{:S(2)}) %collective-permute-start.21) | collective-permute-done | bytes 1048608 | tf_op jit(solution)/shard_map/ppermute | solution.py:63
  120.7 32.1 %all_to_all.18 = bf16[8,256,256]{2,1,0:T(8,128)(2,1)S(1)} all-to-all(bf16[8,256,256]{2,1,0:T(8,128)(2,1)S(1)} %bitcast.34), channel_id=1, replica_groups=mesh['y'=4,'zh'=2,'core'=2,'x'=4,'zl'=2] {'y','zh'}, dimensions={0} | all-to-all | bytes 2097152 | tf_op jit(solution)/shard_map/all_to_all | solution.py:641
  155.0 3.3 %weight_terms.5 = bf16[256,2048]{1,0:T(8,128)(2,1)} custom-call(bf16[256,256]{1,0:T(8,128)(2,1)} %copy-done.11, bf16[256,256]{1,0:T(8,128)(2,1)} %copy-done.12, bf16[256,8192]{1,0:T(8,128)(2,1)} %copy-done, bf16[256,8192]{1,0:T(8,128)(2,1)} %copy-done.8), custom_call_target="tpu_custom_call" | custom-call | flops 536870912 | bytes 3145728 | tf_op jit(solution)/shard_map/weight_terms/pallas_call | solution.py:183
  159.6 4.9 %weight_terms.4 = (bf16[256,2048]{1,0:T(8,128)(2,1)}, bf16[256,2048]{1,0:T(8,128)(2,1)}) custom-call(bf16[256,256]{1,0:T(8,128)(2,1)} %copy-done.11, bf16[256,256]{1,0:T(8,128)(2,1)} %copy-done.12, bf16[256,8192]{1,0:T(8,128)(2,1)} %copy-done, bf16[256,8192]{1,0:T(8,128)(2,1)} %copy-done.8), custom_call_target="tpu_custom_call" | custom-call | flops 1073741824 | bytes 6291456 | tf_op jit(solution)/shard_map/weight_terms/pallas_call | solution.py:183
  164.6 3.2 %collective-permute-start.23 = (bf16[256,2048]{1,0:T(8,128)(2,1)}, bf16[256,2048]{1,0:T(8,128)(2,1)}, u32[]{:S(2)}, u32[]{:S(2)}) collective-permute-start(bf16[256,2048]{1,0:T(8,128)(2,1)} %get-tuple-element.39), channel_id=1, source_target_pairs={{0,17},{1,0},{2,19},{3,2},{4,21},{5,4},{6,23},{7,6},{8,14},{9,15},... | collective-permute-start | bytes 3145736 | tf_op jit(solution)/shard_map/ppermute | solution.py:92
  168.2 11.2 %token_gradient.1 = bf16[256,16384]{1,0:T(8,128)(2,1)} custom-call(s32[128]{0:T(128)} %copy-done.5, bf16[256,256]{1,0:T(8,128)(2,1)} %copy-done.11, bf16[2048,256]{1,0:T(8,128)(2,1)} %copy-done.2, bf16[2048,256]{1,0:T(8,128)(2,1)} %copy-done.13, bf16[2048,256]{1,0:T(8,128)(2,1)} %copy-done.14, bf16[2048,256]{1,0:T(8,128)(2,1)} %copy-done.16, ...), custom_call_target="tpu_custom_call" | custom-call | flops 2147483648 | bytes 16777216 | tf_op jit(solution)/shard_map/token_gradient/pallas_call | solution.py:323
  179.4 3.4 %weight_terms.3 = f32[256,2048]{1,0:T(8,128)} custom-call(bf16[256,256]{1,0:T(8,128)(2,1)} %copy-done.11, bf16[256,256]{1,0:T(8,128)(2,1)} %copy-done.12, bf16[256,8192]{1,0:T(8,128)(2,1)} %copy-done, bf16[256,8192]{1,0:T(8,128)(2,1)} %copy-done.8), custom_call_target="tpu_custom_call" | custom-call | flops 536870912 | bytes 3145728 | tf_op jit(solution)/shard_map/weight_terms/pallas_call | solution.py:183
  182.8 3.3 %collective-permute-done.24 = bf16[256,2048]{1,0:T(8,128)(2,1)S(1)} collective-permute-done((bf16[256,2048]{1,0:T(8,128)(2,1)}, bf16[256,2048]{1,0:T(8,128)(2,1)S(1)}, u32[]{:S(2)}, u32[]{:S(2)}) %collective-permute-start.24) | collective-permute-done | bytes 1048608 | tf_op jit(solution)/shard_map/ppermute | solution.py:92
  186.1 2.5 %add_add_fusion = f32[256,2048]{1,0:T(8,128)S(1)} fusion(f32[256,2048]{1,0:T(8,128)} %weight_terms.3, bf16[256,2048]{1,0:T(8,128)(2,1)S(1)} %collective-permute-done.25, bf16[256,2048]{1,0:T(8,128)(2,1)S(1)} %collective-permute-done.24, bf16[256,2048]{1,0:T(8,128)(2,1)} %collective-permute-done.23), kind=kLoop, calls=%fused_computation | loop fusion | flops 3145728 | bytes 7340032 | tf_op jit(solution)/shard_map/add | solution.py:655
  190.8 2.8 %collective-permute-start.26 = (bf16[256,512]{1,0:T(8,128)(2,1)S(1)}, bf16[256,512]{1,0:T(8,128)(2,1)S(1)}, u32[]{:S(2)}, u32[]{:S(2)}) collective-permute-start(bf16[256,512]{1,0:T(8,128)(2,1)S(1)} %get-tuple-element.47), channel_id=1, source_target_pairs={{0,96},{1,97},{2,98},{3,99},{4,100},{5,101},{6,102},{7,103},{8,25}... | collective-permute-start | bytes 786440 | tf_op jit(solution)/shard_map/ppermute | solution.py:92
  194.6 2.3 %collective-permute-done.28 = bf16[256,512]{1,0:T(8,128)(2,1)S(1)} collective-permute-done((bf16[256,512]{1,0:T(8,128)(2,1)S(1)}, bf16[256,512]{1,0:T(8,128)(2,1)S(1)}, u32[]{:S(2)}, u32[]{:S(2)}) %collective-permute-start.28) | collective-permute-done | bytes 262176 | tf_op jit(solution)/shard_map/ppermute | solution.py:92
  196.9 2.7 %collective-permute-done.27 = bf16[256,512]{1,0:T(8,128)(2,1)S(1)} collective-permute-done((bf16[256,512]{1,0:T(8,128)(2,1)S(1)}, bf16[256,512]{1,0:T(8,128)(2,1)S(1)}, u32[]{:S(2)}, u32[]{:S(2)}) %collective-permute-start.27) | collective-permute-done | bytes 262176 | tf_op jit(solution)/shard_map/ppermute | solution.py:92
  (119 shorter events, 47.5 us)
Async XLA Ops:
  2.2 6.8 %collective-permute-start.2 = (f32[128,256]{1,0:T(8,128)}, f32[128,256]{1,0:T(8,128)S(1)}, u32[]{:S(2)}, u32[]{:S(2)}) collective-permute-start(f32[128,256]{1,0:T(8,128)} %pair_latents.1), channel_id=1, source_target_pairs={{0,4},{1,5},{2,6},{3,7},{4,0},{5,1},{6,2},{7,3},{8,72},{9,73},{10,... | collective-permute-start | bytes 393224 | tf_op jit(solution)/shard_map/ppermute | solution.py:86
  5.4 5.2 %collective-permute-start.1 = (f32[128,256]{1,0:T(8,128)}, f32[128,256]{1,0:T(8,128)S(1)}, u32[]{:S(2)}, u32[]{:S(2)}) collective-permute-start(f32[128,256]{1,0:T(8,128)} %pair_latents.1), channel_id=1, source_target_pairs={{0,6},{1,7},{2,0},{3,1},{4,2},{5,3},{6,4},{7,5},{8,104},{9,105},{1... | collective-permute-start | bytes 393224 | tf_op jit(solution)/shard_map/ppermute | solution.py:86
  6.5 6.4 %collective-permute-start = (f32[128,256]{1,0:T(8,128)}, f32[128,256]{1,0:T(8,128)S(1)}, u32[]{:S(2)}, u32[]{:S(2)}) collective-permute-start(f32[128,256]{1,0:T(8,128)} %pair_latents.1), channel_id=1, source_target_pairs={{0,2},{1,3},{2,4},{3,5},{4,6},{5,7},{6,0},{7,1},{8,40},{9,41},{10,... | collective-permute-start | bytes 393224 | tf_op jit(solution)/shard_map/ppermute | solution.py:86
  8.8 11.9 %collective-permute-start.3 = (bf16[256,1024]{1,0:T(8,128)(2,1)S(1)}, bf16[256,1024]{1,0:T(8,128)(2,1)S(1)}, u32[]{:S(2)}, u32[]{:S(2)}) collective-permute-start(bf16[256,1024]{1,0:T(8,128)(2,1)S(1)} %pad_maximum_fusion.1), channel_id=1, source_target_pairs={{0,8},{1,9},{2,10},{3,11},{4,12},{5,13},{6,14},{7,15},{8,0},{9,1},... | collective-permute-start | bytes 1572872 | tf_op jit(solution)/shard_map/ppermute | solution.py:63
  13.8 10.5 %collective-permute-start.4 = (f32[512,256]{1,0:T(8,128)S(1)}, f32[512,256]{1,0:T(8,128)S(1)}, u32[]{:S(2)}, u32[]{:S(2)}) collective-permute-start(f32[512,256]{1,0:T(8,128)S(1)} %pad_maximum_fusion.refs_0_), channel_id=1, source_target_pairs={{0,32},{1,33},{2,34},{3,35},{4,36},{5,37},{6,38},{7,39},{8,9},{9,2... | collective-permute-start | bytes 1572872 | tf_op jit(solution)/shard_map/ppermute | solution.py:86
  15.5 9.2 %collective-permute-start.5 = (f32[512,256]{1,0:T(8,128)S(1)}, f32[512,256]{1,0:T(8,128)S(1)}, u32[]{:S(2)}, u32[]{:S(2)}) collective-permute-start(f32[512,256]{1,0:T(8,128)S(1)} %pad_maximum_fusion.refs_0_), channel_id=1, source_target_pairs={{0,96},{1,97},{2,98},{3,99},{4,100},{5,101},{6,102},{7,103},{8,25}... | collective-permute-start | bytes 1572872 | tf_op jit(solution)/shard_map/ppermute | solution.py:86
  17.1 14.0 %collective-permute-start.6 = (f32[512,256]{1,0:T(8,128)S(1)}, f32[512,256]{1,0:T(8,128)S(1)}, u32[]{:S(2)}, u32[]{:S(2)}) collective-permute-start(f32[512,256]{1,0:T(8,128)S(1)} %pad_maximum_fusion.refs_0_), channel_id=1, source_target_pairs={{0,64},{1,65},{2,66},{3,67},{4,68},{5,69},{6,70},{7,71},{8,24},{9,... | collective-permute-start | bytes 1572872 | tf_op jit(solution)/shard_map/ppermute | solution.py:86
  31.3 6.0 %collective-permute-start.9 = (f32[8,256]{1,0:T(8,128)S(1)}, f32[8,256]{1,0:T(8,128)S(1)}, u32[]{:S(2)}, u32[]{:S(2)}) collective-permute-start(f32[8,256]{1,0:T(8,128)S(1)} %magnitudes.1), channel_id=1, source_target_pairs={{0,16},{1,17},{2,18},{3,19},{4,20},{5,21},{6,22},{7,23},{8,12},{9,... | collective-permute-start | bytes 24584 | tf_op jit(solution)/shard_map/ppermute | solution.py:86
  36.0 4.9 %collective-permute-start.7 = (f32[8,256]{1,0:T(8,128)S(1)}, f32[8,256]{1,0:T(8,128)S(1)}, u32[]{:S(2)}, u32[]{:S(2)}) collective-permute-start(f32[8,256]{1,0:T(8,128)S(1)} %magnitudes.1), channel_id=1, source_target_pairs={{0,1},{1,16},{2,3},{3,18},{4,5},{5,20},{6,7},{7,22},{8,10},{9,11},... | collective-permute-start | bytes 24584 | tf_op jit(solution)/shard_map/ppermute | solution.py:86
  43.1 27.3 %collective-permute-start.12 = (bf16[2048,256]{1,0:T(8,128)(2,1)S(1)}, bf16[2048,256]{1,0:T(8,128)(2,1)S(1)}, u32[]{:S(2)}, u32[]{:S(2)}) collective-permute-start(bf16[2048,256]{1,0:T(8,128)(2,1)S(1)} %ternarize.1.rest_0_), channel_id=1, source_target_pairs={{0,1},{1,16},{2,3},{3,18},{4,5},{5,20},{6,7},{7,22},{8,10},{9,11},... | collective-permute-start | bytes 3145736 | tf_op jit(solution)/shard_map/ppermute | solution.py:86
  43.2 27.2 %collective-permute-start.14 = (bf16[2048,256]{1,0:T(8,128)(2,1)S(1)}, bf16[2048,256]{1,0:T(8,128)(2,1)S(1)}, u32[]{:S(2)}, u32[]{:S(2)}) collective-permute-start(bf16[2048,256]{1,0:T(8,128)(2,1)S(1)} %ternarize.1.rest_0_), channel_id=1, source_target_pairs={{0,17},{1,0},{2,19},{3,2},{4,21},{5,4},{6,23},{7,6},{8,14},{9,15},... | collective-permute-start | bytes 3145736 | tf_op jit(solution)/shard_map/ppermute | solution.py:86
  46.4 24.5 %collective-permute-start.11 = (bf16[2048,256]{1,0:T(8,128)(2,1)S(1)}, bf16[2048,256]{1,0:T(8,128)(2,1)S(1)}, u32[]{:S(2)}, u32[]{:S(2)}) collective-permute-start(bf16[2048,256]{1,0:T(8,128)(2,1)S(1)} %ternarize.1.rest_0_), channel_id=1, source_target_pairs={{0,8},{1,9},{2,10},{3,11},{4,12},{5,13},{6,14},{7,15},{8,0},{9,1},... | collective-permute-start | bytes 3145736 | tf_op jit(solution)/shard_map/ppermute | solution.py:63
  46.4 25.0 %collective-permute-start.16 = (bf16[2048,256]{1,0:T(8,128)(2,1)S(1)}, bf16[2048,256]{1,0:T(8,128)(2,1)S(1)}, u32[]{:S(2)}, u32[]{:S(2)}) collective-permute-start(bf16[2048,256]{1,0:T(8,128)(2,1)S(1)} %ternarize.1.rest_0_), channel_id=1, source_target_pairs={{0,16},{1,17},{2,18},{3,19},{4,20},{5,21},{6,22},{7,23},{8,12},{9,... | collective-permute-start | bytes 3145736 | tf_op jit(solution)/shard_map/ppermute | solution.py:86
  54.8 63.0 %collective-permute-start.20 = (bf16[256,8192]{1,0:T(8,128)(2,1)S(1)}, bf16[256,8192]{1,0:T(8,128)(2,1)S(1)}, u32[]{:S(2)}, u32[]{:S(2)}) collective-permute-start(bf16[256,8192]{1,0:T(8,128)(2,1)S(1)} %get-tuple-element.31), channel_id=1, source_target_pairs={{0,8},{1,9},{2,10},{3,11},{4,12},{5,13},{6,14},{7,15},{8,0},{9,1},... | collective-permute-start | bytes 12582920 | tf_op jit(solution)/shard_map/ppermute | solution.py:63
  71.4 4.7 %collective-permute-start.17 = (bf16[2048,256]{1,0:T(8,128)(2,1)S(1)}, bf16[2048,256]{1,0:T(8,128)(2,1)S(1)}, u32[]{:S(2)}, u32[]{:S(2)}) collective-permute-start(bf16[2048,256]{1,0:T(8,128)(2,1)S(1)} %collective-permute-done.16.rest_3_), channel_id=1, source_target_pairs={{0,8},{1,9},{2,10},{3,11},{4,12},{5,13},{6,14},{7,15},{8,0},{9,1},... | collective-permute-start | bytes 3145736 | tf_op jit(solution)/shard_map/ppermute | solution.py:63
  158.3 24.5 %collective-permute-start.25 = (bf16[256,2048]{1,0:T(8,128)(2,1)}, bf16[256,2048]{1,0:T(8,128)(2,1)S(1)}, u32[]{:S(2)}, u32[]{:S(2)}) collective-permute-start(bf16[256,2048]{1,0:T(8,128)(2,1)} %weight_terms.5), channel_id=1, source_target_pairs={{0,16},{1,17},{2,18},{3,19},{4,20},{5,21},{6,22},{7,23},{8,12},{9,... | collective-permute-start | bytes 3145736 | tf_op jit(solution)/shard_map/ppermute | solution.py:92
  164.5 21.7 %collective-permute-start.24 = (bf16[256,2048]{1,0:T(8,128)(2,1)}, bf16[256,2048]{1,0:T(8,128)(2,1)S(1)}, u32[]{:S(2)}, u32[]{:S(2)}) collective-permute-start(bf16[256,2048]{1,0:T(8,128)(2,1)} %get-tuple-element.40), channel_id=1, source_target_pairs={{0,1},{1,16},{2,3},{3,18},{4,5},{5,20},{6,7},{7,22},{8,10},{9,11},... | collective-permute-start | bytes 3145736 | tf_op jit(solution)/shard_map/ppermute | solution.py:92
  164.6 21.6 %collective-permute-start.23 = (bf16[256,2048]{1,0:T(8,128)(2,1)}, bf16[256,2048]{1,0:T(8,128)(2,1)}, u32[]{:S(2)}, u32[]{:S(2)}) collective-permute-start(bf16[256,2048]{1,0:T(8,128)(2,1)} %get-tuple-element.39), channel_id=1, source_target_pairs={{0,17},{1,0},{2,19},{3,2},{4,21},{5,4},{6,23},{7,6},{8,14},{9,15},... | collective-permute-start | bytes 3145736 | tf_op jit(solution)/shard_map/ppermute | solution.py:92
  167.9 25.7 %collective-permute-start.19 = (bf16[256,1024]{1,0:T(8,128)(2,1)S(1)}, bf16[256,1024]{1,0:T(8,128)(2,1)S(1)}, u32[]{:S(2)}, u32[]{:S(2)}) collective-permute-start(bf16[256,1024]{1,0:T(8,128)(2,1)S(1)} %pad_maximum_fusion.2), channel_id=1, source_target_pairs={{0,8},{1,9},{2,10},{3,11},{4,12},{5,13},{6,14},{7,15},{8,0},{9,1},... | collective-permute-start | bytes 1572872 | tf_op jit(solution)/shard_map/ppermute | solution.py:63
  188.8 8.1 %collective-permute-start.28 = (bf16[256,512]{1,0:T(8,128)(2,1)S(1)}, bf16[256,512]{1,0:T(8,128)(2,1)S(1)}, u32[]{:S(2)}, u32[]{:S(2)}) collective-permute-start(bf16[256,512]{1,0:T(8,128)(2,1)S(1)} %get-tuple-element.48), channel_id=1, source_target_pairs={{0,64},{1,65},{2,66},{3,67},{4,68},{5,69},{6,70},{7,71},{8,24},{9,... | collective-permute-start | bytes 786440 | tf_op jit(solution)/shard_map/ppermute | solution.py:92
  190.4 9.2 %collective-permute-start.27 = (bf16[256,512]{1,0:T(8,128)(2,1)S(1)}, bf16[256,512]{1,0:T(8,128)(2,1)S(1)}, u32[]{:S(2)}, u32[]{:S(2)}) collective-permute-start(bf16[256,512]{1,0:T(8,128)(2,1)S(1)} %get-tuple-element.49), channel_id=1, source_target_pairs={{0,32},{1,33},{2,34},{3,35},{4,36},{5,37},{6,38},{7,39},{8,9},{9,2... | collective-permute-start | bytes 786440 | tf_op jit(solution)/shard_map/ppermute | solution.py:92
  190.8 8.8 %collective-permute-start.26 = (bf16[256,512]{1,0:T(8,128)(2,1)S(1)}, bf16[256,512]{1,0:T(8,128)(2,1)S(1)}, u32[]{:S(2)}, u32[]{:S(2)}) collective-permute-start(bf16[256,512]{1,0:T(8,128)(2,1)S(1)} %get-tuple-element.47), channel_id=1, source_target_pairs={{0,96},{1,97},{2,98},{3,99},{4,100},{5,101},{6,102},{7,103},{8,25}... | collective-permute-start | bytes 786440 | tf_op jit(solution)/shard_map/ppermute | solution.py:92
  200.5 5.5 %collective-permute-start.30 = (bf16[256,128]{1,0:T(8,128)(2,1)S(1)}, bf16[256,128]{1,0:T(8,128)(2,1)S(1)}, u32[]{:S(2)}, u32[]{:S(2)}) collective-permute-start(bf16[256,128]{1,0:T(8,128)(2,1)S(1)} %get-tuple-element.57), channel_id=1, source_target_pairs={{0,2},{1,3},{2,4},{3,5},{4,6},{5,7},{6,0},{7,1},{8,40},{9,41},{10,... | collective-permute-start | bytes 196616 | tf_op jit(solution)/shard_map/ppermute | solution.py:92
  201.9 5.8 %collective-permute-start.31 = (bf16[256,128]{1,0:T(8,128)(2,1)S(1)}, bf16[256,128]{1,0:T(8,128)(2,1)S(1)}, u32[]{:S(2)}, u32[]{:S(2)}) collective-permute-start(bf16[256,128]{1,0:T(8,128)(2,1)S(1)} %get-tuple-element.56), channel_id=1, source_target_pairs={{0,4},{1,5},{2,6},{3,7},{4,0},{5,1},{6,2},{7,3},{8,72},{9,73},{10,... | collective-permute-start | bytes 196616 | tf_op jit(solution)/shard_map/ppermute | solution.py:92
  (26 other events, 206.5 us)

commit v2 on v1

--- a/solution.py
+++ b/solution.py
@@ -346,16 +346,15 @@
 
 
 def attention_kernel(
-    meta, queries, cotangent, peer_both, kv_same, kv_other,
+    meta, q_columns, c_columns, q_rows, c_rows, kv_same, kv_other,
     mixed_out, query_grad, same_out, other_out,
-    q_held, c_held, peer_held, kv_held, key_acc, value_acc, scores, prob_grad, low,
-    q_columns, c_columns, q_rows, c_rows, sems,
+    kv_held, key_acc, value_acc, scores, prob_grad, low, sems,
     *, heads, head_size, block, docs, blocks,
 ):
     scale = head_size ** (-0.5)
     columns = heads * block
     ctx, core = meta[docs + blocks], meta[docs + blocks + 1]
-    own_blocks = q_held.shape[0] // block
+    own_blocks = q_rows.shape[0] // 2
     in_strip = lax.broadcasted_iota(jnp.int32, (STRIP, columns), 0)
     sides = ((kv_same, core, same_out), (kv_other, 1 - core, other_out))
 
@@ -365,41 +364,19 @@
     def true_block(core_of, j):
         return meta[docs + ((j // 2) * 2 + core_of) * 2 + j % 2]
 
-    copies = [
-        pltpu.make_async_copy(source, held, sems.at[n])
-        for n, (source, held) in enumerate(
-            ((queries, q_held), (cotangent, c_held), (peer_both, peer_held))
-        )
-    ]
-    for copy in copies:
-        copy.start()
     for n, (ref, core_of, _) in enumerate(sides):
         for j in range(blocks // 2):
             pltpu.make_async_copy(
                 ref.at[j * block : (j + 1) * block, :],
                 kv_held.at[rows_at(true_block(core_of, j) + 1, block), :],
-                sems.at[len(copies) + n],
+                sems.at[n],
             ).start()
     kv_held[:block, :] = jnp.zeros((block, 2 * head_size), kv_held.dtype)
     key_acc[...] = jnp.zeros_like(key_acc)
     value_acc[...] = jnp.zeros_like(value_acc)
-    for copy in copies:
-        copy.wait()
-    for i in range(2 * own_blocks):
-        here = slice(i % own_blocks * block, (i % own_blocks + 1) * block)
-        for h in range(heads):
-            part = slice(h * block, (h + 1) * block)
-            if i < own_blocks:
-                head = rows_at(core * heads + h, head_size)
-                q, c = q_held[here, head], c_held[here, head]
-            else:
-                q = peer_held[here, h * head_size : (h + 1) * head_size]
-                c = peer_held[here, (heads + h) * head_size : (heads + h + 1) * head_size]
-            q_rows[i, part, :], c_rows[i, part, :] = q, c
-            q_columns[i, :, part], c_columns[i, :, part] = q.T, c.T
     for n, (ref, _, _) in enumerate(sides):
         pltpu.make_async_copy(
-            ref, kv_held.at[: blocks // 2 * block, :], sems.at[len(copies) + n]
+            ref, kv_held.at[: blocks // 2 * block, :], sems.at[n]
         ).wait()
 
     def chunk_rows(last, c):
@@ -513,13 +490,52 @@
             out[part, head_size:] = value_acc[source, :].astype(out.dtype)
 
 
-def attention(meta, queries, cotangent, peer_both, kv_same, kv_other, head_size, docs, blocks):
+def arrange_kernel(core_of, queries, cotangent, peer_both, q_columns, c_columns, q_rows, c_rows):
+    total, columns, head_size = q_rows.shape
+    own_blocks = total // 2
+    block = queries.shape[0] // own_blocks
+    heads = columns // block
+    for i in range(total):
+        here = slice(i % own_blocks * block, (i % own_blocks + 1) * block)
+        for h in range(heads):
+            part = slice(h * block, (h + 1) * block)
+            if i < own_blocks:
+                at = pl.multiple_of((core_of[0] * heads + h) * head_size, head_size)
+                head = pl.ds(at, head_size)
+                q, c = queries[here, head], cotangent[here, head]
+            else:
+                q = peer_both[here, h * head_size : (h + 1) * head_size]
+                c = peer_both[here, (heads + h) * head_size : (heads + h + 1) * head_size]
+            q_rows[i, part, :], c_rows[i, part, :] = q, c
+            q_columns[i, :, part], c_columns[i, :, part] = q.T, c.T
+
+
+def arrange(core, queries, cotangent, peer_both, head_size, block):
     rows, width = queries.shape
-    heads = width // head_size // 2
+    columns = width // head_size // 2 * block
+    count = 2 * rows // block
+    across = jax.ShapeDtypeStruct((count, head_size, columns), queries.dtype)
+    along = jax.ShapeDtypeStruct((count, columns, head_size), queries.dtype)
+    in_vmem = pl.BlockSpec(memory_space=pltpu.VMEM)
+    return pl.pallas_call(
+        arrange_kernel,
+        out_shape=(across, across, along, along),
+        in_specs=[pl.BlockSpec(memory_space=pltpu.SMEM)] + [in_vmem] * 3,
+        out_specs=(in_vmem,) * 4,
+        compiler_params=pltpu.CompilerParams(vmem_limit_bytes=16 << 20),
+        cost_estimate=pl.CostEstimate(
+            flops=0, bytes_accessed=14 * rows * width, transcendentals=0
+        ),
+        name="arrange_heads",
+    )(core, queries, cotangent, peer_both)
+
+
+def attention(meta, arranged, kv_same, kv_other, head_size, docs, blocks):
     length = kv_same.shape[0] + kv_other.shape[0]
     block = length // blocks
-    columns = heads * block
-    query_blocks = 2 * rows // block
+    query_blocks, _, columns = arranged[0].shape
+    heads = columns // block
+    rows, width = query_blocks * block // 2, 2 * heads * head_size
     in_vmem = pl.BlockSpec(memory_space=pltpu.VMEM)
     most_chunks = 10
     visible = 9 * KEY_CHUNK
@@ -533,23 +549,18 @@
             jax.ShapeDtypeStruct(kv_same.shape, jnp.float32),
             jax.ShapeDtypeStruct(kv_other.shape, jnp.bfloat16),
         ),
-        in_specs=[pl.BlockSpec(memory_space=pltpu.SMEM)] + [pl.BlockSpec(memory_space=pl.ANY)] * 5,
+        in_specs=[pl.BlockSpec(memory_space=pltpu.SMEM)]
+        + [in_vmem] * 4
+        + [pl.BlockSpec(memory_space=pl.ANY)] * 2,
         out_specs=(in_vmem,) * 4,
         scratch_shapes=[
-            pltpu.VMEM(queries.shape, jnp.bfloat16),
-            pltpu.VMEM(cotangent.shape, jnp.bfloat16),
-            pltpu.VMEM(peer_both.shape, jnp.bfloat16),
             pltpu.VMEM((block + length, 2 * head_size), jnp.bfloat16),
             pltpu.VMEM((block + length, head_size), jnp.float32),
             pltpu.VMEM((block + length, head_size), jnp.float32),
             pltpu.VMEM((most_chunks, KEY_CHUNK, columns), jnp.float32),
             pltpu.VMEM((KEY_CHUNK, columns), jnp.float32),
             pltpu.VMEM((2, KEY_CHUNK, columns), jnp.bfloat16),
-            pltpu.VMEM((query_blocks, head_size, columns), jnp.bfloat16),
-            pltpu.VMEM((query_blocks, head_size, columns), jnp.bfloat16),
-            pltpu.VMEM((query_blocks, columns, head_size), jnp.bfloat16),
-            pltpu.VMEM((query_blocks, columns, head_size), jnp.bfloat16),
-            pltpu.SemaphoreType.DMA((5,)),
+            pltpu.SemaphoreType.DMA((2,)),
         ],
         compiler_params=pltpu.CompilerParams(vmem_limit_bytes=26 << 20),
         cost_estimate=pl.CostEstimate(
@@ -558,7 +569,7 @@
             transcendentals=2 * rows * heads * visible,
         ),
         name="masked_attention",
-    )(meta, queries, cotangent, peer_both, kv_same, kv_other)
+    )(meta, *arranged, kv_same, kv_other)
 
 
 def body(tokens, queries, cotangent, latent_key, latent_value, lengths, block_order):
@@ -592,6 +603,8 @@
     latents = side_by_side(latent_key, latent_value)
     latents = gather_ring(jnp.concatenate(gather_ring(latents, 0), axis=0), 1)
     latents[0], peer_both, meta = lax.optimization_barrier((latents[0], peer_both, meta))
+    block = rows_here * lax.axis_size(CTX) // blocks
+    arranged = arrange(meta[-1:], queries[0], cotangent[0], peer_both, head_size, block)
     sums = small(
         magnitudes_kernel,
         "magnitudes",
@@ -620,6 +633,7 @@
                 rows[:, cut], part, preferred_element_type=jnp.float32
             )
     kv_here = projected.astype(jnp.bfloat16)
+    kv_here, arranged = lax.optimization_barrier((kv_here, arranged))
     groups = lax.axis_size(SAME_CORE_CTX)
     kv_same = lax.all_to_all(
         jnp.broadcast_to(kv_here[None], (groups,) + kv_here.shape).reshape(-1, 2 * head_size),
@@ -632,7 +646,7 @@
     tokens_peer = swap_cores(tokens_other)
 
     mixed, query_grad, same_terms, other_terms = attention(
-        meta, queries[0], cotangent[0], peer_both, kv_same, kv_other, head_size, docs, blocks
+        meta, arranged, kv_same, kv_other, head_size, docs, blocks
     )
     same_terms, other_terms, tokens_peer = lax.optimization_barrier(
         (same_terms, other_terms, tokens_peer)

time: 208 us -> 206 us (level)
  waiting for transfers between devices: 54.7 us -> 48.4 us
  blocking collectives: 52.3 us -> 46.7 us
  Pallas kernels: 48.1 us -> 53.3 us
  local copies, waits for them, and re-layouts: 7.63 us -> 10 us
  starting transfers between devices: 33.6 us -> 35.8 us
    all_to_all x1, blocking collectives: 32.1 us -> 26.4 us  [body(): lax.all_to_all(chip_terms, SAME_CORE_CTX, split_axis=0, concat_axis=0, ti...]
    pallas_call x1, Pallas kernels: 17.7 us -> 21.7 us  [attention(): pl.pallas_call(functools.partial(attention_kernel, heads=heads, head_size...]
    ppermute x12, waiting for transfers between devices: 32.9 us -> 28.9 us  [gather_ring(): lax.ppermute(value, AXES, along_ring(phase, -offset))]
    ppermute x9, starting transfers between devices: 11.6 us -> 14 us  [sent_along_ring(): lax.ppermute(piece.astype(jnp.bfloat16), AXES, along_ring(phase, offset))]
    ppermute x9, waiting for transfers between devices: 13.1 us -> 10.8 us  [sent_along_ring(): lax.ppermute(piece.astype(jnp.bfloat16), AXES, along_ring(phase, offset))]
  transfers between devices with their start and end apart: 32 -> 32, of which waited for: 21 -> 20; matrix products, arithmetic and copies ran while one was open for 6% -> 6% of each run, Pallas kernels for 20% -> 23%
where the time goes in v2:
time: 206 us
  Pallas kernels  53.3 us (26%)
  waiting for transfers between devices  48.4 us (23%)
  blocking collectives  46.7 us (23%)
  starting transfers between devices  35.8 us (17%)
  local copies, waits for them, and re-layouts  10 us (5%)
  other arithmetic  7.49 us (4%)
  matrix products  3.48 us (2%)
    ppermute x12, waiting for transfers between devices, gather_ring(): lax.ppermute(value, AXES, along_ring(phase, -offset))  28.9 us
    all_to_all x1, blocking collectives, body(): lax.all_to_all(chip_terms, SAME_CORE_CTX, split_axis=0, concat_axis=0, ti...  26.4 us
    pallas_call x1, Pallas kernels, attention(): pl.pallas_call(functools.partial(attention_kernel, heads=heads, head_size...  21.7 us
    ppermute x12, starting transfers between devices, gather_ring(): lax.ppermute(value, AXES, along_ring(phase, -offset))  20.5 us
    all_to_all x1, blocking collectives, body(): lax.all_to_all(jnp.broadcast_to(kv_here[None], (groups,) + kv_here.shape)...  20.2 us
    ppermute x9, starting transfers between devices, sent_along_ring(): lax.ppermute(piece.astype(jnp.bfloat16), AXES, along_ring(phase, offset))  14 us
    pallas_call x3, Pallas kernels, weight_terms(): pl.pallas_call(functools.partial(weight_terms_kernel, first=first * width...  11.7 us
    pallas_call x1, Pallas kernels, token_gradient(): pl.pallas_call(functools.partial(token_grad_kernel, count=len(weights)),...  11.2 us
  transfers between devices with their start and end apart: 32, of which 20 were waited for; matrix products, arithmetic and copies ran while one was open for 6% of the time, Pallas kernels for 23%

profile of v2, /device:TPU:0, one launch (start us, length us, event | category | flops | bytes accessed | tf_op | source)
XLA Modules:
  0.0 206.3 jit_solution(11796297625327453855)
XLA Ops:
  2.2 3.2 %collective-permute-start.2 = (f32[128,256]{1,0:T(8,128)}, f32[128,256]{1,0:T(8,128)S(1)}, u32[]{:S(2)}, u32[]{:S(2)}) collective-permute-start(f32[128,256]{1,0:T(8,128)} %pair_latents.1), channel_id=1, source_target_pairs={{0,4},{1,5},{2,6},{3,7},{4,0},{5,1},{6,2},{7,3},{8,72},{9,73},{10,... | collective-permute-start | bytes 393224 | tf_op jit(solution)/shard_map/ppermute | solution.py:86
  10.5 2.4 %collective-permute-done = f32[128,256]{1,0:T(8,128)S(1)} collective-permute-done((f32[128,256]{1,0:T(8,128)}, f32[128,256]{1,0:T(8,128)S(1)}, u32[]{:S(2)}, u32[]{:S(2)}) %collective-permute-start) | collective-permute-done | bytes 131104 | tf_op jit(solution)/shard_map/ppermute | solution.py:86
  20.6 3.7 %collective-permute-done.4.refs_1_ = f32[512,256]{1,0:T(8,128)S(1)} collective-permute-done((f32[512,256]{1,0:T(8,128)S(1)}, f32[512,256]{1,0:T(8,128)S(1)}, u32[]{:S(2)}, u32[]{:S(2)}) %collective-permute-start.4) | collective-permute-done | bytes 524320 | tf_op jit(solution)/shard_map/ppermute | solution.py:86
  24.7 6.5 %collective-permute-done.6.refs_3_ = f32[512,256]{1,0:T(8,128)S(1)} collective-permute-done((f32[512,256]{1,0:T(8,128)S(1)}, f32[512,256]{1,0:T(8,128)S(1)}, u32[]{:S(2)}, u32[]{:S(2)}) %collective-permute-start.6) | collective-permute-done | bytes 524320 | tf_op jit(solution)/shard_map/ppermute | solution.py:86
  31.3 4.0 %collective-permute-start.9 = (f32[8,256]{1,0:T(8,128)S(1)}, f32[8,256]{1,0:T(8,128)S(1)}, u32[]{:S(2)}, u32[]{:S(2)}) collective-permute-start(f32[8,256]{1,0:T(8,128)S(1)} %magnitudes.1), channel_id=1, source_target_pairs={{0,16},{1,17},{2,18},{3,19},{4,20},{5,21},{6,22},{7,23},{8,12},{9,... | collective-permute-start | bytes 24584 | tf_op jit(solution)/shard_map/ppermute | solution.py:86
  43.3 3.1 %collective-permute-start.14 = (bf16[2048,256]{1,0:T(8,128)(2,1)S(1)}, bf16[2048,256]{1,0:T(8,128)(2,1)S(1)}, u32[]{:S(2)}, u32[]{:S(2)}) collective-permute-start(bf16[2048,256]{1,0:T(8,128)(2,1)S(1)} %ternarize.1.rest_0_), channel_id=1, source_target_pairs={{0,17},{1,0},{2,19},{3,2},{4,21},{5,4},{6,23},{7,6},{8,14},{9,15},... | collective-permute-start | bytes 3145736 | tf_op jit(solution)/shard_map/ppermute | solution.py:86
  52.0 3.4 %copy-done.1 = bf16[1,256,16384]{2,1,0:T(8,128)(2,1)S(1)} copy-done((bf16[1,256,16384]{2,1,0:T(8,128)(2,1)S(1)}, bf16[1,256,16384]{2,1,0:T(8,128)(2,1)}, u32[]{:S(2)}) %copy-start.1) | copy-done | bytes 8388632
  55.3 4.2 %shuffle_tokens.1 = (bf16[256,8192]{1,0:T(8,128)(2,1)S(1)}, bf16[256,8192]{1,0:T(8,128)(2,1)S(1)}) custom-call(s32[128]{0:T(128)S(1)} %fusion.14.table, bf16[256,16384]{1,0:T(8,128)(2,1)S(1)} %bitcast.28), custom_call_target="tpu_custom_call" | custom-call | bytes 16777216 | tf_op jit(solution)/shard_map/shuffle_tokens/pallas_call | solution.py:116
  59.7 10.7 %collective-permute-done.12.rest_1_ = bf16[2048,256]{1,0:T(8,128)(2,1)S(1)} collective-permute-done((bf16[2048,256]{1,0:T(8,128)(2,1)S(1)}, bf16[2048,256]{1,0:T(8,128)(2,1)S(1)}, u32[]{:S(2)}, u32[]{:S(2)}) %collective-permute-start.12) | collective-permute-done | bytes 1048608 | tf_op jit(solution)/shard_map/ppermute | solution.py:86
  76.6 20.2 %all_to_all.17 = bf16[8,256,256]{2,1,0:T(8,128)(2,1)S(1)} all-to-all(bf16[8,256,256]{2,1,0:T(8,128)(2,1)S(1)} %broadcast_in_dim.32), channel_id=1, replica_groups=mesh['y'=4,'zh'=2,'core'=2,'x'=4,'zl'=2] {'y','zh'}, dimensions={0} | all-to-all | bytes 2097152 | tf_op jit(solution)/shard_map/all_to_all | solution.py:638
  96.8 2.7 %collective-permute-done.18.kv_other = bf16[2048,256]{1,0:T(8,128)(2,1)S(1)} collective-permute-done((bf16[2048,256]{1,0:T(8,128)(2,1)S(1)}, bf16[2048,256]{1,0:T(8,128)(2,1)S(1)}, u32[]{:S(2)}, u32[]{:S(2)}) %collective-permute-start.18) | collective-permute-done | bytes 1048608 | tf_op jit(solution)/shard_map/ppermute | solution.py:63
  99.5 21.7 %masked_attention.1 = (bf16[512,512]{1,0:T(8,128)(2,1)S(1)}, bf16[512,512]{1,0:T(8,128)(2,1)S(1)}, f32[2048,256]{1,0:T(8,128)S(1)}, bf16[2048,256]{1,0:T(8,128)(2,1)S(1)}) custom-call(s32[42]{0:T(128)S(1)} %pad_add_fusion.meta, bf16[4,128,512]{2,1,0:T(8,128)(2,1)S(1)} %get-tuple-element.45.q_columns, bf16[4,128,512]{2,1,0:T(8,128)(2,1)S(1)} %get-tuple-element.46.c_columns, ...), custom_call_target="tpu_custom_call" | custom-call | flops 8455716864 | bytes 6291456 | tf_op jit(solution)/shard_map/masked_attention/pallas_call | solution.py:542
  121.4 2.5 %collective-permute-done.21 = bf16[2048,256]{1,0:T(8,128)(2,1)S(1)} collective-permute-done((bf16[2048,256]{1,0:T(8,128)(2,1)S(1)}, bf16[2048,256]{1,0:T(8,128)(2,1)S(1)}, u32[]{:S(2)}, u32[]{:S(2)}) %collective-permute-start.21) | collective-permute-done | bytes 1048608 | tf_op jit(solution)/shard_map/ppermute | solution.py:63
  124.2 26.4 %all_to_all.18 = bf16[8,256,256]{2,1,0:T(8,128)(2,1)S(1)} all-to-all(bf16[8,256,256]{2,1,0:T(8,128)(2,1)S(1)} %bitcast.34), channel_id=1, replica_groups=mesh['y'=4,'zh'=2,'core'=2,'x'=4,'zl'=2] {'y','zh'}, dimensions={0} | all-to-all | bytes 2097152 | tf_op jit(solution)/shard_map/all_to_all | solution.py:655
  152.9 3.3 %weight_terms.5 = bf16[256,2048]{1,0:T(8,128)(2,1)} custom-call(bf16[256,256]{1,0:T(8,128)(2,1)} %copy-done.11, bf16[256,256]{1,0:T(8,128)(2,1)} %copy-done.12, bf16[256,8192]{1,0:T(8,128)(2,1)} %copy-done, bf16[256,8192]{1,0:T(8,128)(2,1)} %copy-done.8), custom_call_target="tpu_custom_call" | custom-call | flops 536870912 | bytes 3145728 | tf_op jit(solution)/shard_map/weight_terms/pallas_call | solution.py:183
  157.5 4.9 %weight_terms.4 = (bf16[256,2048]{1,0:T(8,128)(2,1)}, bf16[256,2048]{1,0:T(8,128)(2,1)}) custom-call(bf16[256,256]{1,0:T(8,128)(2,1)} %copy-done.11, bf16[256,256]{1,0:T(8,128)(2,1)} %copy-done.12, bf16[256,8192]{1,0:T(8,128)(2,1)} %copy-done, bf16[256,8192]{1,0:T(8,128)(2,1)} %copy-done.8), custom_call_target="tpu_custom_call" | custom-call | flops 1073741824 | bytes 6291456 | tf_op jit(solution)/shard_map/weight_terms/pallas_call | solution.py:183
  162.4 3.2 %collective-permute-start.23 = (bf16[256,2048]{1,0:T(8,128)(2,1)}, bf16[256,2048]{1,0:T(8,128)(2,1)}, u32[]{:S(2)}, u32[]{:S(2)}) collective-permute-start(bf16[256,2048]{1,0:T(8,128)(2,1)} %get-tuple-element.57), channel_id=1, source_target_pairs={{0,17},{1,0},{2,19},{3,2},{4,21},{5,4},{6,23},{7,6},{8,14},{9,15},... | collective-permute-start | bytes 3145736 | tf_op jit(solution)/shard_map/ppermute | solution.py:92
  165.9 11.2 %token_gradient.1 = bf16[256,16384]{1,0:T(8,128)(2,1)} custom-call(s32[128]{0:T(128)} %copy-done.7, bf16[256,256]{1,0:T(8,128)(2,1)} %copy-done.11, bf16[2048,256]{1,0:T(8,128)(2,1)} %copy-done.2, bf16[2048,256]{1,0:T(8,128)(2,1)} %copy-done.13, bf16[2048,256]{1,0:T(8,128)(2,1)} %copy-done.14, bf16[2048,256]{1,0:T(8,128)(2,1)} %copy-done.16, ...), custom_call_target="tpu_custom_call" | custom-call | flops 2147483648 | bytes 16777216 | tf_op jit(solution)/shard_map/token_gradient/pallas_call | solution.py:323
  177.1 3.5 %weight_terms.3 = f32[256,2048]{1,0:T(8,128)} custom-call(bf16[256,256]{1,0:T(8,128)(2,1)} %copy-done.11, bf16[256,256]{1,0:T(8,128)(2,1)} %copy-done.12, bf16[256,8192]{1,0:T(8,128)(2,1)} %copy-done, bf16[256,8192]{1,0:T(8,128)(2,1)} %copy-done.8), custom_call_target="tpu_custom_call" | custom-call | flops 536870912 | bytes 3145728 | tf_op jit(solution)/shard_map/weight_terms/pallas_call | solution.py:183
  180.6 3.4 %collective-permute-done.24 = bf16[256,2048]{1,0:T(8,128)(2,1)S(1)} collective-permute-done((bf16[256,2048]{1,0:T(8,128)(2,1)}, bf16[256,2048]{1,0:T(8,128)(2,1)S(1)}, u32[]{:S(2)}, u32[]{:S(2)}) %collective-permute-start.24) | collective-permute-done | bytes 1048608 | tf_op jit(solution)/shard_map/ppermute | solution.py:92
  184.0 2.5 %add_add_fusion = f32[256,2048]{1,0:T(8,128)S(1)} fusion(f32[256,2048]{1,0:T(8,128)} %weight_terms.3, bf16[256,2048]{1,0:T(8,128)(2,1)S(1)} %collective-permute-done.25, bf16[256,2048]{1,0:T(8,128)(2,1)S(1)} %collective-permute-done.24, bf16[256,2048]{1,0:T(8,128)(2,1)} %collective-permute-done.23), kind=kLoop, calls=%fused_computation | loop fusion | flops 3145728 | bytes 7340032 | tf_op jit(solution)/shard_map/add | solution.py:669
  188.7 2.8 %collective-permute-start.26 = (bf16[256,512]{1,0:T(8,128)(2,1)S(1)}, bf16[256,512]{1,0:T(8,128)(2,1)S(1)}, u32[]{:S(2)}, u32[]{:S(2)}) collective-permute-start(bf16[256,512]{1,0:T(8,128)(2,1)S(1)} %get-tuple-element.65), channel_id=1, source_target_pairs={{0,96},{1,97},{2,98},{3,99},{4,100},{5,101},{6,102},{7,103},{8,25}... | collective-permute-start | bytes 786440 | tf_op jit(solution)/shard_map/ppermute | solution.py:92
  194.8 2.7 %collective-permute-done.27 = bf16[256,512]{1,0:T(8,128)(2,1)S(1)} collective-permute-done((bf16[256,512]{1,0:T(8,128)(2,1)S(1)}, bf16[256,512]{1,0:T(8,128)(2,1)S(1)}, u32[]{:S(2)}, u32[]{:S(2)}) %collective-permute-start.27) | collective-permute-done | bytes 262176 | tf_op jit(solution)/shard_map/ppermute | solution.py:92
  199.8 2.5 %collective-permute-start.31 = (bf16[256,128]{1,0:T(8,128)(2,1)S(1)}, bf16[256,128]{1,0:T(8,128)(2,1)S(1)}, u32[]{:S(2)}, u32[]{:S(2)}) collective-permute-start(bf16[256,128]{1,0:T(8,128)(2,1)S(1)} %get-tuple-element.74), channel_id=1, source_target_pairs={{0,4},{1,5},{2,6},{3,7},{4,0},{5,1},{6,2},{7,3},{8,72},{9,73},{10,... | collective-permute-start | bytes 196616 | tf_op jit(solution)/shard_map/ppermute | solution.py:92
  (121 shorter events, 50.5 us)
Async XLA Ops:
  2.2 6.8 %collective-permute-start.2 = (f32[128,256]{1,0:T(8,128)}, f32[128,256]{1,0:T(8,128)S(1)}, u32[]{:S(2)}, u32[]{:S(2)}) collective-permute-start(f32[128,256]{1,0:T(8,128)} %pair_latents.1), channel_id=1, source_target_pairs={{0,4},{1,5},{2,6},{3,7},{4,0},{5,1},{6,2},{7,3},{8,72},{9,73},{10,... | collective-permute-start | bytes 393224 | tf_op jit(solution)/shard_map/ppermute | solution.py:86
  5.4 5.2 %collective-permute-start.1 = (f32[128,256]{1,0:T(8,128)}, f32[128,256]{1,0:T(8,128)S(1)}, u32[]{:S(2)}, u32[]{:S(2)}) collective-permute-start(f32[128,256]{1,0:T(8,128)} %pair_latents.1), channel_id=1, source_target_pairs={{0,6},{1,7},{2,0},{3,1},{4,2},{5,3},{6,4},{7,5},{8,104},{9,105},{1... | collective-permute-start | bytes 393224 | tf_op jit(solution)/shard_map/ppermute | solution.py:86
  6.5 6.4 %collective-permute-start = (f32[128,256]{1,0:T(8,128)}, f32[128,256]{1,0:T(8,128)S(1)}, u32[]{:S(2)}, u32[]{:S(2)}) collective-permute-start(f32[128,256]{1,0:T(8,128)} %pair_latents.1), channel_id=1, source_target_pairs={{0,2},{1,3},{2,4},{3,5},{4,6},{5,7},{6,0},{7,1},{8,40},{9,41},{10,... | collective-permute-start | bytes 393224 | tf_op jit(solution)/shard_map/ppermute | solution.py:86
  8.8 11.9 %collective-permute-start.3 = (bf16[256,1024]{1,0:T(8,128)(2,1)S(1)}, bf16[256,1024]{1,0:T(8,128)(2,1)S(1)}, u32[]{:S(2)}, u32[]{:S(2)}) collective-permute-start(bf16[256,1024]{1,0:T(8,128)(2,1)S(1)} %pad_maximum_fusion.1), channel_id=1, source_target_pairs={{0,8},{1,9},{2,10},{3,11},{4,12},{5,13},{6,14},{7,15},{8,0},{9,1},... | collective-permute-start | bytes 1572872 | tf_op jit(solution)/shard_map/ppermute | solution.py:63
  13.8 10.5 %collective-permute-start.4 = (f32[512,256]{1,0:T(8,128)S(1)}, f32[512,256]{1,0:T(8,128)S(1)}, u32[]{:S(2)}, u32[]{:S(2)}) collective-permute-start(f32[512,256]{1,0:T(8,128)S(1)} %pad_maximum_fusion.refs_0_), channel_id=1, source_target_pairs={{0,32},{1,33},{2,34},{3,35},{4,36},{5,37},{6,38},{7,39},{8,9},{9,2... | collective-permute-start | bytes 1572872 | tf_op jit(solution)/shard_map/ppermute | solution.py:86
  15.5 9.2 %collective-permute-start.5 = (f32[512,256]{1,0:T(8,128)S(1)}, f32[512,256]{1,0:T(8,128)S(1)}, u32[]{:S(2)}, u32[]{:S(2)}) collective-permute-start(f32[512,256]{1,0:T(8,128)S(1)} %pad_maximum_fusion.refs_0_), channel_id=1, source_target_pairs={{0,96},{1,97},{2,98},{3,99},{4,100},{5,101},{6,102},{7,103},{8,25}... | collective-permute-start | bytes 1572872 | tf_op jit(solution)/shard_map/ppermute | solution.py:86
  17.1 14.0 %collective-permute-start.6 = (f32[512,256]{1,0:T(8,128)S(1)}, f32[512,256]{1,0:T(8,128)S(1)}, u32[]{:S(2)}, u32[]{:S(2)}) collective-permute-start(f32[512,256]{1,0:T(8,128)S(1)} %pad_maximum_fusion.refs_0_), channel_id=1, source_target_pairs={{0,64},{1,65},{2,66},{3,67},{4,68},{5,69},{6,70},{7,71},{8,24},{9,... | collective-permute-start | bytes 1572872 | tf_op jit(solution)/shard_map/ppermute | solution.py:86
  31.3 6.0 %collective-permute-start.9 = (f32[8,256]{1,0:T(8,128)S(1)}, f32[8,256]{1,0:T(8,128)S(1)}, u32[]{:S(2)}, u32[]{:S(2)}) collective-permute-start(f32[8,256]{1,0:T(8,128)S(1)} %magnitudes.1), channel_id=1, source_target_pairs={{0,16},{1,17},{2,18},{3,19},{4,20},{5,21},{6,22},{7,23},{8,12},{9,... | collective-permute-start | bytes 24584 | tf_op jit(solution)/shard_map/ppermute | solution.py:86
  36.0 4.9 %collective-permute-start.7 = (f32[8,256]{1,0:T(8,128)S(1)}, f32[8,256]{1,0:T(8,128)S(1)}, u32[]{:S(2)}, u32[]{:S(2)}) collective-permute-start(f32[8,256]{1,0:T(8,128)S(1)} %magnitudes.1), channel_id=1, source_target_pairs={{0,1},{1,16},{2,3},{3,18},{4,5},{5,20},{6,7},{7,22},{8,10},{9,11},... | collective-permute-start | bytes 24584 | tf_op jit(solution)/shard_map/ppermute | solution.py:86
  43.1 27.3 %collective-permute-start.12 = (bf16[2048,256]{1,0:T(8,128)(2,1)S(1)}, bf16[2048,256]{1,0:T(8,128)(2,1)S(1)}, u32[]{:S(2)}, u32[]{:S(2)}) collective-permute-start(bf16[2048,256]{1,0:T(8,128)(2,1)S(1)} %ternarize.1.rest_0_), channel_id=1, source_target_pairs={{0,1},{1,16},{2,3},{3,18},{4,5},{5,20},{6,7},{7,22},{8,10},{9,11},... | collective-permute-start | bytes 3145736 | tf_op jit(solution)/shard_map/ppermute | solution.py:86
  43.3 27.2 %collective-permute-start.14 = (bf16[2048,256]{1,0:T(8,128)(2,1)S(1)}, bf16[2048,256]{1,0:T(8,128)(2,1)S(1)}, u32[]{:S(2)}, u32[]{:S(2)}) collective-permute-start(bf16[2048,256]{1,0:T(8,128)(2,1)S(1)} %ternarize.1.rest_0_), channel_id=1, source_target_pairs={{0,17},{1,0},{2,19},{3,2},{4,21},{5,4},{6,23},{7,6},{8,14},{9,15},... | collective-permute-start | bytes 3145736 | tf_op jit(solution)/shard_map/ppermute | solution.py:86
  46.4 24.5 %collective-permute-start.11 = (bf16[2048,256]{1,0:T(8,128)(2,1)S(1)}, bf16[2048,256]{1,0:T(8,128)(2,1)S(1)}, u32[]{:S(2)}, u32[]{:S(2)}) collective-permute-start(bf16[2048,256]{1,0:T(8,128)(2,1)S(1)} %ternarize.1.rest_0_), channel_id=1, source_target_pairs={{0,8},{1,9},{2,10},{3,11},{4,12},{5,13},{6,14},{7,15},{8,0},{9,1},... | collective-permute-start | bytes 3145736 | tf_op jit(solution)/shard_map/ppermute | solution.py:63
  46.4 25.0 %collective-permute-start.16 = (bf16[2048,256]{1,0:T(8,128)(2,1)S(1)}, bf16[2048,256]{1,0:T(8,128)(2,1)S(1)}, u32[]{:S(2)}, u32[]{:S(2)}) collective-permute-start(bf16[2048,256]{1,0:T(8,128)(2,1)S(1)} %ternarize.1.rest_0_), channel_id=1, source_target_pairs={{0,16},{1,17},{2,18},{3,19},{4,20},{5,21},{6,22},{7,23},{8,12},{9,... | collective-permute-start | bytes 3145736 | tf_op jit(solution)/shard_map/ppermute | solution.py:86
  59.6 61.6 %collective-permute-start.20 = (bf16[256,8192]{1,0:T(8,128)(2,1)S(1)}, bf16[256,8192]{1,0:T(8,128)(2,1)S(1)}, u32[]{:S(2)}, u32[]{:S(2)}) collective-permute-start(bf16[256,8192]{1,0:T(8,128)(2,1)S(1)} %get-tuple-element.39), channel_id=1, source_target_pairs={{0,8},{1,9},{2,10},{3,11},{4,12},{5,13},{6,14},{7,15},{8,0},{9,1},... | collective-permute-start | bytes 12582920 | tf_op jit(solution)/shard_map/ppermute | solution.py:63
  156.2 24.4 %collective-permute-start.25 = (bf16[256,2048]{1,0:T(8,128)(2,1)}, bf16[256,2048]{1,0:T(8,128)(2,1)S(1)}, u32[]{:S(2)}, u32[]{:S(2)}) collective-permute-start(bf16[256,2048]{1,0:T(8,128)(2,1)} %weight_terms.5), channel_id=1, source_target_pairs={{0,16},{1,17},{2,18},{3,19},{4,20},{5,21},{6,22},{7,23},{8,12},{9,... | collective-permute-start | bytes 3145736 | tf_op jit(solution)/shard_map/ppermute | solution.py:92
  162.4 21.7 %collective-permute-start.24 = (bf16[256,2048]{1,0:T(8,128)(2,1)}, bf16[256,2048]{1,0:T(8,128)(2,1)S(1)}, u32[]{:S(2)}, u32[]{:S(2)}) collective-permute-start(bf16[256,2048]{1,0:T(8,128)(2,1)} %get-tuple-element.58), channel_id=1, source_target_pairs={{0,1},{1,16},{2,3},{3,18},{4,5},{5,20},{6,7},{7,22},{8,10},{9,11},... | collective-permute-start | bytes 3145736 | tf_op jit(solution)/shard_map/ppermute | solution.py:92
  162.4 21.6 %collective-permute-start.23 = (bf16[256,2048]{1,0:T(8,128)(2,1)}, bf16[256,2048]{1,0:T(8,128)(2,1)}, u32[]{:S(2)}, u32[]{:S(2)}) collective-permute-start(bf16[256,2048]{1,0:T(8,128)(2,1)} %get-tuple-element.57), channel_id=1, source_target_pairs={{0,17},{1,0},{2,19},{3,2},{4,21},{5,4},{6,23},{7,6},{8,14},{9,15},... | collective-permute-start | bytes 3145736 | tf_op jit(solution)/shard_map/ppermute | solution.py:92
  165.8 25.7 %collective-permute-start.19 = (bf16[256,1024]{1,0:T(8,128)(2,1)S(1)}, bf16[256,1024]{1,0:T(8,128)(2,1)S(1)}, u32[]{:S(2)}, u32[]{:S(2)}) collective-permute-start(bf16[256,1024]{1,0:T(8,128)(2,1)S(1)} %pad_maximum_fusion.2), channel_id=1, source_target_pairs={{0,8},{1,9},{2,10},{3,11},{4,12},{5,13},{6,14},{7,15},{8,0},{9,1},... | collective-permute-start | bytes 1572872 | tf_op jit(solution)/shard_map/ppermute | solution.py:63
  186.7 8.1 %collective-permute-start.28 = (bf16[256,512]{1,0:T(8,128)(2,1)S(1)}, bf16[256,512]{1,0:T(8,128)(2,1)S(1)}, u32[]{:S(2)}, u32[]{:S(2)}) collective-permute-start(bf16[256,512]{1,0:T(8,128)(2,1)S(1)} %get-tuple-element.66), channel_id=1, source_target_pairs={{0,64},{1,65},{2,66},{3,67},{4,68},{5,69},{6,70},{7,71},{8,24},{9,... | collective-permute-start | bytes 786440 | tf_op jit(solution)/shard_map/ppermute | solution.py:92
  188.2 9.2 %collective-permute-start.27 = (bf16[256,512]{1,0:T(8,128)(2,1)S(1)}, bf16[256,512]{1,0:T(8,128)(2,1)S(1)}, u32[]{:S(2)}, u32[]{:S(2)}) collective-permute-start(bf16[256,512]{1,0:T(8,128)(2,1)S(1)} %get-tuple-element.67), channel_id=1, source_target_pairs={{0,32},{1,33},{2,34},{3,35},{4,36},{5,37},{6,38},{7,39},{8,9},{9,2... | collective-permute-start | bytes 786440 | tf_op jit(solution)/shard_map/ppermute | solution.py:92
  188.7 8.8 %collective-permute-start.26 = (bf16[256,512]{1,0:T(8,128)(2,1)S(1)}, bf16[256,512]{1,0:T(8,128)(2,1)S(1)}, u32[]{:S(2)}, u32[]{:S(2)}) collective-permute-start(bf16[256,512]{1,0:T(8,128)(2,1)S(1)} %get-tuple-element.65), channel_id=1, source_target_pairs={{0,96},{1,97},{2,98},{3,99},{4,100},{5,101},{6,102},{7,103},{8,25}... | collective-permute-start | bytes 786440 | tf_op jit(solution)/shard_map/ppermute | solution.py:92
  197.7 5.5 %collective-permute-start.29 = (bf16[256,128]{1,0:T(8,128)(2,1)S(1)}, bf16[256,128]{1,0:T(8,128)(2,1)S(1)}, u32[]{:S(2)}, u32[]{:S(2)}) collective-permute-start(bf16[256,128]{1,0:T(8,128)(2,1)S(1)} %get-tuple-element.76), channel_id=1, source_target_pairs={{0,6},{1,7},{2,0},{3,1},{4,2},{5,3},{6,4},{7,5},{8,104},{9,105},{1... | collective-permute-start | bytes 196616 | tf_op jit(solution)/shard_map/ppermute | solution.py:92
  197.8 5.5 %collective-permute-start.30 = (bf16[256,128]{1,0:T(8,128)(2,1)S(1)}, bf16[256,128]{1,0:T(8,128)(2,1)S(1)}, u32[]{:S(2)}, u32[]{:S(2)}) collective-permute-start(bf16[256,128]{1,0:T(8,128)(2,1)S(1)} %get-tuple-element.75), channel_id=1, source_target_pairs={{0,2},{1,3},{2,4},{3,5},{4,6},{5,7},{6,0},{7,1},{8,40},{9,41},{10,... | collective-permute-start | bytes 196616 | tf_op jit(solution)/shard_map/ppermute | solution.py:92
  199.8 5.8 %collective-permute-start.31 = (bf16[256,128]{1,0:T(8,128)(2,1)S(1)}, bf16[256,128]{1,0:T(8,128)(2,1)S(1)}, u32[]{:S(2)}, u32[]{:S(2)}) collective-permute-start(bf16[256,128]{1,0:T(8,128)(2,1)S(1)} %get-tuple-element.74), channel_id=1, source_target_pairs={{0,4},{1,5},{2,6},{3,7},{4,0},{5,1},{6,2},{7,3},{8,72},{9,73},{10,... | collective-permute-start | bytes 196616 | tf_op jit(solution)/shard_map/ppermute | solution.py:92
  (26 other events, 171.4 us)
